TPU v7x, 32 devices: a whole 2x2x4 slice. The times are simulated.
32 devices in a mesh: groups: 2 (over x), row: 16 (over z, y, core).
Axes of the slice: x: 2, y: 2, z: 4, core: 2. Of those that a mesh axis runs over, the one named last changes fastest.
Arguments:
- forcing: bfloat16 [16, 32, 512, 256], P(None, None, ('groups', 'row')), parts along dimension 2, may hold values from -6 to 6
- rainfall: float32 [512, 256], P(('groups', 'row')), parts along dimension 0, may hold values from 0.05 to 3
- depth_start: float32 [512, 256], P(('groups', 'row')), parts along dimension 0, may hold values from 0.2 to 2
- observed: float32 [512, 256], P(('groups', 'row')), parts along dimension 0, may hold values from -3.8 to 5.8
- land_mask: int32 [256, 256], P('row'), may hold values from 0 to 1, as said below
- tile_land: int32 [16], replicated, may hold values from 0 to 4096, as said below
- land_rank: int32 [256, 256], P('row'), may hold values from -1 to 4095, as said below
- flow_code: int32 [256, 256], P('row'), may hold values from 0 to 7
- terrain_slope: float32 [256, 256], P('row'), may hold values from 0.01 to 0.3
- input_weight: bfloat16 [256, 32], replicated, may hold values from -1 to 1
- hidden_weight: bfloat16 [256, 64], replicated, may hold values from -0.75 to 0.75
- gate_bias: float32 [256], replicated, may hold values from -3 to 3
- head_weight: float32 [2, 64], replicated, may hold values from -2.4 to 2.4
- head_offset: float32 [2], replicated, may hold values from -1 to 1
Outputs:
- depth_final: float32 [512, 256], P(('groups', 'row')), parts along dimension 0
- misfit: float32 [2], P('groups'), parts along dimension 0
- input_grad: float32 [512, 32], P('groups'), parts along dimension 0
- hidden_grad: float32 [512, 64], P('groups'), parts along dimension 0
- bias_grad: float32 [512], P('groups'), parts along dimension 0
- head_grad: float32 [4, 64], P('groups'), parts along dimension 0
- offset_grad: float32 [4], P('groups'), parts along dimension 0
There are 2 independent parts, one for each index of `groups`. A program takes and returns all parts, laid end to end along the dimension named above; an argument that names none is the same for every part. Nothing has to cross between parts.
Inputs may be any that keep to these rules, and one draw needn't show every extreme that they name: `tile_land`: the counts sum to 32768; some band holds 4096 land cells and some band none. `land_mask`: band t has exactly tile_land[t] cells equal to 1. `land_rank`: in band t the land cells (land_mask 1) carry 0 .. tile_land[t] - 1, each once; sea cells carry -1.
All inputs are finite; a program needn't handle non-finite values.
Results may differ from a plain program's by a relative error of at most 0.00089.
Values may be sent and summed in bfloat16 or wider, within the bound.
No kernel may reach another device: no remote copies, remote signals or barrier semaphores. Data moves between devices by JAX's collectives and lax.ppermute only.
A program may use at most 192 MiB of HBM per device.

v0:
```python
from functools import partial

import jax
import jax.numpy as jnp
from jax import lax
from jax.sharding import PartitionSpec as P

SUB = 6
LAND_DEV = 2048


compass = ((-1, -1), (-1, 0), (-1, 1), (0, -1), (0, 1), (1, -1), (1, 0), (1, 1))


def with_halo(cells, sides, width):
    for axis, dim in sides:
        count = lax.axis_size(axis)
        ends = count - 1
        head = lax.slice_in_dim(cells, 0, width, axis=dim)
        tail = lax.slice_in_dim(cells, cells.shape[dim] - width, cells.shape[dim], axis=dim)
        cells = jnp.concatenate(
            [
                lax.ppermute(tail, axis, [(i, (i + 1) % count) for i in range(ends)]),
                cells,
                lax.ppermute(head, axis, [((i + 1) % count, i) for i in range(ends)]),
            ],
            axis=dim,
        )
    return cells


def cell_forward(input_weight, hidden_weight, gate_bias, inputs):
    hidden_size = hidden_weight.shape[1]
    cell_count = inputs.shape[2]

    def advance(carry, inputs_now):
        state_low, memory, state = carry
        summed = jnp.dot(input_weight, inputs_now, preferred_element_type=jnp.float32)
        summed = (
            summed
            + jnp.dot(hidden_weight, state_low, preferred_element_type=jnp.float32)
            + gate_bias[:, None]
        )
        gate_in = jax.nn.sigmoid(summed[:hidden_size])
        gate_keep = jax.nn.sigmoid(summed[hidden_size : 2 * hidden_size])
        candidate = jnp.tanh(summed[2 * hidden_size : 3 * hidden_size])
        gate_out = jax.nn.sigmoid(summed[3 * hidden_size :])
        memory_new = gate_keep * memory + gate_in * candidate
        state_new = gate_out * jnp.tanh(memory_new)
        gate_values = jnp.concatenate([gate_in, gate_keep, candidate, gate_out], axis=0)
        return (
            (state_new.astype(jnp.bfloat16), memory_new, state_new),
            (gate_values, memory_new, state_low),
        )

    start_carry = (
        jnp.zeros((hidden_size, cell_count), jnp.bfloat16),
        jnp.zeros((hidden_size, cell_count), jnp.float32),
        jnp.zeros((hidden_size, cell_count), jnp.float32),
    )
    final_carry, stash = lax.scan(advance, start_carry, inputs)
    return (final_carry[2], stash)


def cell_backward(hidden_weight, inputs, stash, grad_hidden):
    gate_values, memories, states_low = stash
    hidden_size = hidden_weight.shape[1]
    feat_count = inputs.shape[1]
    earlier = jnp.concatenate([jnp.zeros_like(memories[:1]), memories[:-1]], axis=0)
    contract_cells = (((1,), (1,)), ((), ()))

    def retreat(carry, item):
        grad_state, grad_memory, sum_input, sum_hidden, sum_bias = carry
        inputs_now, gate_now, memory_before, memory_now, state_before = item
        gate_in = gate_now[:hidden_size]
        gate_keep = gate_now[hidden_size : 2 * hidden_size]
        candidate = gate_now[2 * hidden_size : 3 * hidden_size]
        gate_out = gate_now[3 * hidden_size :]
        squash = jnp.tanh(memory_now)
        grad_memory = grad_memory + grad_state * gate_out * (1.0 - squash * squash)
        grad_summed = jnp.concatenate(
            [
                grad_memory * candidate * gate_in * (1.0 - gate_in),
                grad_memory * memory_before * gate_keep * (1.0 - gate_keep),
                grad_memory * gate_in * (1.0 - candidate * candidate),
                grad_state * squash * gate_out * (1.0 - gate_out),
            ],
            axis=0,
        )
        rounded = grad_summed.astype(jnp.bfloat16)
        sum_input = sum_input + lax.dot_general(
            rounded, inputs_now, contract_cells, preferred_element_type=jnp.float32
        )
        sum_hidden = sum_hidden + lax.dot_general(
            rounded, state_before, contract_cells, preferred_element_type=jnp.float32
        )
        sum_bias = sum_bias + jnp.sum(grad_summed, axis=1)
        grad_state = lax.dot_general(
            hidden_weight, rounded, (((0,), (0,)), ((), ())), preferred_element_type=jnp.float32
        )
        grad_memory = grad_memory * gate_keep
        return ((grad_state, grad_memory, sum_input, sum_hidden, sum_bias), None)

    start_carry = (
        grad_hidden,
        jnp.zeros_like(grad_hidden),
        jnp.zeros((4 * hidden_size, feat_count), jnp.float32),
        jnp.zeros((4 * hidden_size, hidden_size), jnp.float32),
        jnp.zeros((4 * hidden_size,), jnp.float32),
    )
    final_carry, _ = lax.scan(
        retreat, start_carry, (inputs, gate_values, earlier, memories, states_low), reverse=True
    )
    return (final_carry[2], final_carry[3], final_carry[4])


def head_params(head_weight, head_offset, hidden):
    act = jnp.dot(head_weight, hidden, precision=lax.Precision.HIGHEST) + head_offset[:, None]
    manning = 0.03 + 0.27 * jax.nn.sigmoid(act[0])
    infiltration = jax.nn.softplus(act[1])
    return jnp.stack([manning, infiltration], axis=0)


def wet_and_out(water_level, infiltration, manning, rainfall, land_frac, root_slope, step_hours):
    wet_depth = (
        land_frac * (water_level + step_hours * rainfall) * jnp.exp(-step_hours * infiltration)
    )
    drain_rate = step_hours * root_slope * (wet_depth + 0.001) ** (2.0 / 3.0) / manning
    return (wet_depth, wet_depth * (1.0 - jnp.exp(-drain_rate)))


def arrivals(padded):
    row_count = padded.shape[1] - 2
    col_count = padded.shape[2]
    framed = jnp.pad(padded, ((0, 0), (0, 0), (1, 1)))
    incoming = jnp.zeros((row_count, col_count), padded.dtype)
    for direction, (row_step, col_step) in enumerate(compass):
        incoming = (
            incoming
            + framed[
                direction,
                1 - row_step : 1 - row_step + row_count,
                1 - col_step : 1 - col_step + col_count,
            ]
        )
    return incoming


def settle(wet_depth, outflow, padded, land_frac):
    return land_frac * (wet_depth - outflow + arrivals(padded))


def fit_term(water_level, observed, land_frac, land_total):
    mismatch = land_frac * (water_level - observed)
    return jnp.sum(mismatch * mismatch) / land_total


def trade_edges(edges):
    return with_halo(edges, (("row", 1),), 1)


def attach(flows):
    edges = jnp.stack([flows[:, 0], flows[:, -1]], axis=1)
    rimmed = trade_edges(edges)
    return jnp.concatenate([rimmed[:, 0:1], flows, rimmed[:, 3:4]], axis=1)


def detach(grad_padded):
    edges = jnp.stack([grad_padded[:, 0], grad_padded[:, -1]], axis=1)
    rimmed = trade_edges(edges)
    inner = grad_padded[:, 1:-1]
    inner = inner.at[:, 0].add(rimmed[:, 0])
    inner = inner.at[:, -1].add(rimmed[:, 3])
    return inner


def shards(
    forcing,
    rainfall,
    depth_start,
    observed,
    land_mask,
    tile_land,
    land_rank,
    flow_code,
    terrain_slope,
    input_weight,
    hidden_weight,
    gate_bias,
    head_weight,
    head_offset,
):
    peers = lax.axis_size("row")
    myself = lax.axis_index("row")
    steps_count, feat_count, row_count, col_count = forcing.shape
    cell_count = row_count * col_count
    capacity = 2 * LAND_DEV
    slot_count = capacity // peers
    land_total = LAND_DEV * peers
    offsets = jnp.cumsum(tile_land) - tile_land
    tile_ends = offsets + tile_land
    own_start = offsets[myself]
    flat_rank = land_rank.reshape(cell_count)
    flat_forcing = forcing.reshape(steps_count * feat_count, cell_count)
    local_order = jnp.where(flat_rank >= 0, flat_rank, capacity)
    cell_of_order = (
        jnp.zeros((capacity,), jnp.int32)
        .at[local_order]
        .set(jnp.arange(cell_count, dtype=jnp.int32), mode="drop")
    )
    slot_ids = jnp.arange(capacity, dtype=jnp.int32)
    target_dev = slot_ids // slot_count
    slot_place = slot_ids % slot_count
    order_of_slot = (target_dev - own_start) % peers + slot_place * peers
    cell_order = jnp.where(flat_rank >= 0, flat_rank, 0)
    packed = jnp.take(flat_forcing, jnp.take(cell_of_order, order_of_slot), axis=1)
    received = lax.all_to_all(packed, "row", split_axis=1, concat_axis=1, tiled=True)
    owned = jnp.arange(LAND_DEV, dtype=jnp.int32) * peers + myself
    source_tile = jnp.sum((tile_ends[None, :] <= owned[:, None]).astype(jnp.int32), axis=1)
    pick_index = source_tile * slot_count + (owned - offsets[source_tile]) // peers
    cell_inputs = jnp.take(received, pick_index, axis=1).reshape(steps_count, feat_count, LAND_DEV)
    hidden, stash = cell_forward(input_weight, hidden_weight, gate_bias, cell_inputs)
    cell_params, head_pull = jax.vjp(head_params, head_weight, head_offset, hidden)
    return_tile = slot_ids // slot_count
    global_index = (
        offsets[return_tile] + (myself - offsets[return_tile]) % peers + slot_place * peers
    )
    is_valid = global_index < tile_ends[return_tile]
    owner_slot = jnp.where(is_valid, global_index // peers, 0)
    outgoing = jnp.where(is_valid[None, :], jnp.take(cell_params, owner_slot, axis=1), 0.0)
    returned = lax.all_to_all(outgoing, "row", split_axis=1, concat_axis=1, tiled=True)
    cell_slot = (own_start + cell_order) % peers * slot_count + cell_order // peers

    def to_grid(slot_params):
        picked = jnp.take(slot_params, cell_slot, axis=1).reshape(2, row_count, col_count)
        return (
            jnp.where(land_mask == 1, picked[0], 0.1),
            jnp.where(land_mask == 1, picked[1], 1.0),
        )

    (manning, infiltration), grid_pull = jax.vjp(to_grid, returned)
    land_frac = land_mask.astype(jnp.float32)
    direction_mask = (flow_code[None] == jnp.arange(8, dtype=jnp.int32)[:, None, None]).astype(
        jnp.float32
    )
    root_slope = jnp.sqrt(terrain_slope)
    step_hours = 1.0 / SUB
    first_half = partial(
        wet_and_out,
        rainfall=rainfall,
        land_frac=land_frac,
        root_slope=root_slope,
        step_hours=step_hours,
    )
    second_half = partial(settle, land_frac=land_frac)
    water_level = depth_start
    pullbacks = []
    for substep in range(SUB):
        (wet_depth, outflow), first_pull = jax.vjp(first_half, water_level, infiltration, manning)
        padded = attach(outflow[None] * direction_mask)
        water_level, second_pull = jax.vjp(second_half, wet_depth, outflow, padded)
        pullbacks.append((first_pull, second_pull))
    misfit_part, fit_pull = jax.vjp(
        partial(fit_term, observed=observed, land_frac=land_frac, land_total=land_total),
        water_level,
    )
    (grad_level,) = fit_pull(jnp.ones_like(misfit_part))
    grad_infil = jnp.zeros_like(infiltration)
    grad_manning = jnp.zeros_like(manning)
    for first_pull, second_pull in reversed(pullbacks):
        grad_wet, grad_out, grad_padded = second_pull(grad_level)
        grad_out = grad_out + jnp.sum(detach(grad_padded) * direction_mask, axis=0)
        grad_level, infil_part, manning_part = first_pull((grad_wet, grad_out))
        grad_infil = grad_infil + infil_part
        grad_manning = grad_manning + manning_part
    (slot_grads,) = grid_pull((grad_manning, grad_infil))
    arrived = lax.all_to_all(slot_grads, "row", split_axis=1, concat_axis=1, tiled=True)
    cell_grads = jnp.take(arrived, pick_index, axis=1)
    head_part, offset_part, hidden_part = head_pull(cell_grads)
    input_part, recur_part, bias_part = cell_backward(
        hidden_weight, cell_inputs, stash, hidden_part
    )
    totals = lax.psum(
        (input_part, recur_part, bias_part, head_part, offset_part, misfit_part), "row"
    )
    return (
        water_level,
        totals[5].reshape(1),
        totals[0],
        totals[1],
        totals[2],
        totals[3],
        totals[4],
    )


def solution(mesh):
    return jax.shard_map(
        shards,
        mesh=mesh,
        in_specs=(
            P(None, None, ("groups", "row"), None),
            P(("groups", "row"), None),
            P(("groups", "row"), None),
            P(("groups", "row"), None),
            P("row", None),
            P(),
            P("row", None),
            P("row", None),
            P("row", None),
            P(),
            P(),
            P(),
            P(),
            P(),
        ),
        out_specs=(
            P(("groups", "row"), None),
            P("groups"),
            P("groups", None),
            P("groups", None),
            P("groups"),
            P("groups", None),
            P("groups"),
        ),
        check_vma=False,
    )
```

profile of v0, /device:TPU:0, one launch (start us, length us, event | category | flops | bytes accessed | tf_op | source)
XLA Modules:
  0.0 724.6 jit_solution(6471612439359628254)
XLA Ops:
  11.0 15.5 %scatter_custom_fusion = s32[4096]{0:T(1024)S(1)} fusion(s32[4096]{0:T(1024)S(1)} %bitcast.298, s32[4096]{0:T(1024)S(1)} %iota.82, s32[]{:T(128)} %constant.564.clone.1), kind=kCustom, calls=%fused_computation.428 | custom fusion | bytes 16388 | tf_op jit(solution)/shard_map/scatter | solution.py:209
  26.6 23.0 %gather_fusion = s32[4096]{0:T(1024)S(1)} fusion(s32[4096]{0:T(1024)S(1)} %scatter_custom_fusion, s32[4096]{0:T(1024)S(1)} %broadcast_clamp_fusion.3), kind=kCustom, calls=%fused_computation | custom fusion | bytes 49152 | tf_op jit(solution)/shard_map/jit(_take)/gather | solution.py:216
  50.3 6.4 copy.56
  56.7 6.5 copy.44
  63.7 20.1 %gather_fusion.1 = bf16[4096,512]{1,0:T(8,128)(2,1)} fusion(bf16[512,4096]{0,1:T(8,128)(2,1)} %copy.44, s32[4096]{0:T(1024)S(1)} %broadcast_clamp_fusion.2), kind=kCustom, calls=%fused_computation.1 | custom fusion | bytes 8404992 | tf_op jit(solution)/shard_map/jit(_take)/gather | solution.py:216
  87.7 7.6 %all-to-all-start = ((bf16[512,16,256]{0,2,1:T(8,128)(2,1)}), bf16[512,16,256]{0,2,1:T(8,128)(2,1)}, u32[]{:S(2)}, u32[]{:S(2)}) async-start(bf16[512,16,256]{0,2,1:T(8,128)(2,1)} %broadcast_select_fusion.2), calls=%async_computation | async-start | bytes 8388608 | tf_op jit(solution)/shard_map/all_to_all | solution.py:217
  100.2 5.8 select_select_fusion.2
  110.9 5.5 select_select_fusion.1
  121.0 5.8 compare_and_fusion.3
  127.1 45.8 %all-to-all-done = bf16[512,16,256]{0,2,1:T(8,128)(2,1)} async-done(((bf16[512,16,256]{0,2,1:T(8,128)(2,1)}), bf16[512,16,256]{0,2,1:T(8,128)(2,1)}, u32[]{:S(2)}, u32[]{:S(2)}) %all-to-all-start) | async-done | bytes 4194336 | tf_op jit(solution)/shard_map/all_to_all | solution.py:217
  172.9 10.3 %gather_fusion.2 = bf16[2048,512]{1,0:T(8,128)(2,1)S(1)} fusion(bf16[512,4096]{0,1:T(8,128)(2,1)} %bitcast.44, s32[2048]{0:T(1024)S(1)} %broadcast_clamp_fusion.4), kind=kCustom, calls=%fused_computation.2 | custom fusion | bytes 4202496 | tf_op jit(solution)/shard_map/jit(_take)/gather | solution.py:221
  188.9 109.9 %while.56 = (s32[]{:T(128)}, bf16[64,2048]{1,0:T(8,128)(2,1)S(1)}, f32[64,2048]{1,0:T(8,128)S(1)}, f32[64,2048]{1,0:T(8,128)}, f32[16,256,2048]{2,1,0:T(8,128)},...) while((s32[]{:T(128)}, bf16[64,2048]{1,0:T(8,128)(2,1)S(1)}, ...), condition=%wide.region_4.5_spmd.clone, body=%wide.region_3.4_spmd.clone.sunk | while | flops 106299392 | bytes 20106376 | solution.py:61
  301.7 12.0 %gather_fusion.3 = f32[4096,2]{1,0:T(8,128)S(1)} fusion(f32[2,2048]{0,1:T(8,128)} %copy.46, s32[4096]{0:T(1024)S(1)} %broadcast_clamp_fusion), kind=kCustom, calls=%fused_computation.3 | custom fusion | bytes 81920 | tf_op jit(solution)/shard_map/jit(_take)/gather | solution.py:230
  315.0 19.6 %all-to-all-start.1 = ((f32[2,16,256]{2,0,1:T(2,128)}), f32[2,16,256]{2,0,1:T(2,128)S(1)}, u32[]{:S(2)}, u32[]{:S(2)}) async-start(f32[2,16,256]{2,0,1:T(2,128)} %select_select_fusion), calls=%async_computation.1 | async-start | bytes 65536 | tf_op jit(solution)/shard_map/all_to_all | solution.py:231
  335.2 6.1 all-to-all-done.1
  341.9 14.1 %gather_fusion.4 = f32[4096,2]{1,0:T(8,128)} fusion(f32[2,4096]{0,1:T(8,128)S(1)} %bitcast.270, s32[4096]{0:T(1024)S(1)} %broadcast_clamp_fusion.1), kind=kCustom, calls=%fused_computation.4 | custom fusion | bytes 81920 | tf_op jit(solution)/shard_map/jvp(jit(_take))/gather | solution.py:235
  382.7 4.7 collective-permute-start.6
  432.6 4.7 collective-permute-start.18
  460.3 23.2 %scatter_custom_fusion.1 = f32[2,4096]{0,1:T(8,128)S(1)} fusion(s32[4096]{0:T(1024)S(1)} %bitcast.290, f32[4096,2]{1,0:T(8,128)} %bitcast.273, f32[]{:T(128)} %constant.579.clone.1), kind=kCustom, calls=%fused_computation.76 | custom fusion | flops 8192 | bytes 33280 | tf_op jit(solution)/shard_map/transpose(jvp(jit(_take)))/scatter-add | solution.py:235
  484.8 12.8 %all-to-all-start.2 = ((f32[2,16,256]{2,0,1:T(2,128)}), f32[2,16,256]{2,0,1:T(2,128)S(1)}, u32[]{:S(2)}, u32[]{:S(2)}) async-start(f32[2,16,256]{2,0,1:T(2,128)} %copy.50), calls=%async_computation.2 | async-start | bytes 65536 | tf_op jit(solution)/shard_map/all_to_all | solution.py:277
  507.9 7.0 gather_fusion.5
  516.0 113.6 %while.57 = (s32[]{:T(128)}, f32[64,2048]{1,0:T(8,128)S(1)}, f32[64,2048]{1,0:T(8,128)S(1)}, f32[256,32]{0,1:T(8,128)S(1)}, f32[256,64]{0,1:T(8,128)S(1)}, /*ind...) while((s32[]{:T(128)}, f32[64,2048]{1,0:T(8,128)S(1)}, ...), condition=%wide.region_16.17_spmd.clone, body=%wide.region_14.16_spmd.clone.sunk | while | flops 177127680 | bytes 17928448 | solution.py:111
  631.0 63.6 %all-reduce.59 = (f32[1]{0:T(128)}, f32[256,32]{0,1:T(8,128)}, f32[256]{0:T(256)}, f32[2,64]{1,0:T(2,128)}, f32[2]{0:T(128)}) all-reduce(f32[1]{0:T(128)} %bitcast.64, f32[256,32]{0,1:T(8,128)S(1)} %get-tuple-element.452, f32[256]{0:T(256)S(1)} %get-tuple-element.454, ...), channel_id=1, replica_groups=mesh['groups'=2,'row'=16] {'row'}, use_global_device_ids=true, to_apply=%region_6.7 | all-reduce | flops 8579 | bytes 68632 | tf_op jit(solution)/shard_map/psum | solution.py:283
  694.6 21.6 %all-reduce.62.cloned.1.call-done = f32[256,64]{0,1:T(8,128)} async-done(((f32[256,64]{0,1:T(8,128)}), f32[256,64]{0,1:T(8,128)}) %all-reduce.62.cloned.1.call-update) | async-done | bytes 65552 | tf_op jit(solution)/shard_map/psum | solution.py:283
  (459 shorter events, 365.1 us)
Async XLA Ops:
  87.7 85.3 %all-to-all-start = ((bf16[512,16,256]{0,2,1:T(8,128)(2,1)}), bf16[512,16,256]{0,2,1:T(8,128)(2,1)}, u32[]{:S(2)}, u32[]{:S(2)}) async-start(bf16[512,16,256]{0,2,1:T(8,128)(2,1)} %broadcast_select_fusion.2), calls=%async_computation | async-start | bytes 8388608 | tf_op jit(solution)/shard_map/all_to_all | solution.py:217
  315.0 26.3 %all-to-all-start.1 = ((f32[2,16,256]{2,0,1:T(2,128)}), f32[2,16,256]{2,0,1:T(2,128)S(1)}, u32[]{:S(2)}, u32[]{:S(2)}) async-start(f32[2,16,256]{2,0,1:T(2,128)} %select_select_fusion), calls=%async_computation.1 | async-start | bytes 65536 | tf_op jit(solution)/shard_map/all_to_all | solution.py:231
  363.1 3.3 collective-permute-start.1
  366.9 5.6 collective-permute-start.2
  371.2 3.1 collective-permute-start.3
  374.6 5.9 collective-permute-start.4
  379.2 3.1 collective-permute-start.5
  382.7 6.1 collective-permute-start.6
  387.4 3.1 collective-permute-start.7
  390.9 6.1 collective-permute-start.8
  395.6 3.1 collective-permute-start.9
  399.1 6.1 collective-permute-start.10
  403.8 3.1 collective-permute-start.11
  407.5 6.2 collective-permute-start.12
  412.3 3.1 collective-permute-start.13
  416.0 6.2 collective-permute-start.14
  420.9 3.1 collective-permute-start.15
  424.3 6.2 collective-permute-start.16
  429.2 3.1 collective-permute-start.17
  432.6 6.2 collective-permute-start.18
  441.0 6.2 collective-permute-start.20
  449.9 6.2 collective-permute-start.22
  484.8 21.1 %all-to-all-start.2 = ((f32[2,16,256]{2,0,1:T(2,128)}), f32[2,16,256]{2,0,1:T(2,128)S(1)}, u32[]{:S(2)}, u32[]{:S(2)}) async-start(f32[2,16,256]{2,0,1:T(2,128)} %copy.50), calls=%async_computation.2 | async-start | bytes 65536 | tf_op jit(solution)/shard_map/all_to_all | solution.py:277
  497.6 218.7 %all-reduce.62.cloned.1.call-start = ((), (), s32[]{:S(2)}) async-start(), calls=%async_computation.3 | async-start | bytes 131072 | tf_op jit(solution)/shard_map/psum | solution.py:283
  (19 other events, 650.1 us)
Sparse Core Ops, SparseCore 0:
  630.4 85.7 all-reduce.61
where the time goes:
time: 728 us; the launch traced here: 725 us
  other arithmetic  218 us (30%)
  local copies, waits for them, and re-layouts  142 us (20%)
  starting transfers between devices  109 us (15%)
  waiting for transfers between devices  93.9 us (13%)
  matrix products  80.5 us (11%)
  blocking collectives  63.6 us (9%)
  between operations  16.1 us (2%)
    psum x1, blocking collectives, shards(): lax.psum((input_part, recur_part, bias_part, head_part, offset_part, misf...  63.6 us
    dynamic_update_slice x48, other arithmetic, cell_forward(): final_carry, stash = lax.scan(advance, start_carry, inputs)  58.6 us
    ppermute x12, starting transfers between devices, with_halo(): lax.ppermute(tail, axis, [(i, (i + 1) % count) for i in range(ends)])  53.2 us
    all_to_all x1, waiting for transfers between devices, shards(): lax.all_to_all(packed, 'row', split_axis=1, concat_axis=1, tiled=True)  45.8 us
    mul x16, other arithmetic, retreat(): grad_memory * candidate * gate_in * (1.0 - gate_in)  29.9 us
    mul x16, other arithmetic, retreat(): grad_memory = grad_memory * gate_keep  28.1 us
    scatter-add x1, other arithmetic, to_grid(): jnp.take(slot_params, cell_slot, axis=1).reshape(2, row_count, col_count)  23.2 us
    gather x2, local copies, waits for them, and re-layouts, shards(): jnp.take(cell_of_order, order_of_slot)  23 us
  transfers between devices with their start and end apart: 28, of which 15 were waited for; matrix products, arithmetic and copies ran while one was open for 6% of the time, Pallas kernels for 0%

commit v1 on v0

v1 whole, which is shorter than its diff:
```python
import jax
import jax.numpy as jnp
from jax import lax
from jax.experimental import pallas as pl
from jax.experimental.pallas import tpu as pltpu
from jax.sharding import PartitionSpec as P

SUB = 6
LAND_DEV = 2048
PAD = 16
EXTRA = 16

compass = ((-1, -1), (-1, 0), (-1, 1), (0, -1), (0, 1), (1, -1), (1, 0), (1, 1))


def forward_kernel(x_ref, perm_ref, w_ref, hwt_ref, off_ref, z_ref, c_ref, act_ref, last_ref, h_scr, c_scr):
    t = pl.program_id(0)
    steps = pl.num_programs(0)
    rows, cols = act_ref.shape[1], act_ref.shape[2]
    hid = c_scr.shape[0]
    feat = perm_ref.shape[0] // rows

    @pl.when(t == 0)
    def _():
        h_scr[...] = jnp.zeros_like(h_scr)
        c_scr[...] = jnp.zeros_like(c_scr)

    moved = jnp.dot(perm_ref[...], x_ref[0], preferred_element_type=jnp.float32).astype(jnp.bfloat16)
    weight = w_ref[...]
    row_id = lax.broadcasted_iota(jnp.int32, (PAD, cols), 0)
    ones = jnp.where(row_id < 3, 1.0, 0.0).astype(jnp.bfloat16)
    for r in range(rows):
        span = slice(r * cols, (r + 1) * cols)
        before = c_scr[:, span]
        state = jnp.concatenate([moved[r * feat:(r + 1) * feat], h_scr[:, span], ones], axis=0)
        z_ref[0, :, span] = state
        c_ref[0, :, span] = before
        gates = jnp.tanh(jnp.dot(weight, state, preferred_element_type=jnp.float32))
        t_in = gates[:hid]
        t_keep = gates[hid:2 * hid]
        cand = gates[2 * hid:3 * hid]
        t_out = gates[3 * hid:]
        memory = 0.5 * ((t_keep + 1.0) * before + (t_in + 1.0) * cand)
        twice = (t_out + 1.0) * jnp.tanh(memory)
        c_scr[:, span] = memory
        h_scr[:, span] = twice.astype(jnp.bfloat16)
        last_ref[:, span] = twice

    @pl.when(t == steps - 1)
    def _():
        for r in range(rows):
            span = slice(r * cols, (r + 1) * cols)
            twice = last_ref[:, span]
            for j in range(2):
                act = jnp.sum(twice * hwt_ref[:, j:j + 1], axis=0, keepdims=True)
                act_ref[j, r:r + 1, :] = act + off_ref[0, j]


def shift_rows(value, step):
    return pltpu.roll(value, step % value.shape[0], 0)


def shift_cols(value, step, col_id):
    cols = value.shape[1]
    moved = pltpu.roll(value, step % cols, 1)
    edge = 0 if step > 0 else cols - 1
    return jnp.where(col_id == edge, 0.0, moved)


def water_kernel(land_total, own_ref, up_ref, dn_ref, act_ref, act_up_ref, act_dn_ref, last_ref, depth_ref, gact_ref, extra_ref):
    rows, cols = depth_ref.shape
    hid = last_ref.shape[0]

    def window(up, own, dn, j):
        return jnp.concatenate([up[j], own[j], dn[j]], axis=0)

    start = window(up_ref, own_ref, dn_ref, 0)
    rain = window(up_ref, own_ref, dn_ref, 1)
    observed = window(up_ref, own_ref, dn_ref, 2)
    root_slope = window(up_ref, own_ref, dn_ref, 3)
    code = window(up_ref, own_ref, dn_ref, 4)
    act0 = window(act_up_ref, act_ref, act_dn_ref, 0)
    act1 = window(act_up_ref, act_ref, act_dn_ref, 1)
    is_land = code > 0.5
    land = jnp.where(is_land, 1.0, 0.0)
    sig0 = 0.5 * jnp.tanh(0.5 * act0) + 0.5
    sig1 = 0.5 * jnp.tanh(0.5 * act1) + 0.5
    soft1 = jnp.maximum(act1, 0.0) + jnp.log(1.0 + jnp.exp(-jnp.abs(act1)))
    manning = jnp.where(is_land, 0.03 + 0.27 * sig0, 0.1)
    infil = jnp.where(is_land, soft1, 1.0)
    dt = 1.0 / SUB
    col_id = lax.broadcasted_iota(jnp.int32, code.shape, 1)
    masks = [jnp.where(code == float(d + 1), 1.0, 0.0) for d in range(8)]
    soak = land * jnp.exp(-dt * infil)
    rain_dt = dt * rain
    rate = dt * root_slope / manning

    def arrive(out):
        total = None
        for col_step in (-1, 0, 1):
            part = None
            for d, (rs, cs) in enumerate(compass):
                if cs != col_step:
                    continue
                flow = out * masks[d]
                flow = shift_rows(flow, rs) if rs else flow
                part = flow if part is None else part + flow
            part = shift_cols(part, col_step, col_id) if col_step else part
            total = part if total is None else total + part
        return total

    def collect(grad):
        total = None
        for col_step in (-1, 0, 1):
            base = shift_cols(grad, -col_step, col_id) if col_step else grad
            for d, (rs, cs) in enumerate(compass):
                if cs != col_step:
                    continue
                back = shift_rows(base, -rs) if rs else base
                back = back * masks[d]
                total = back if total is None else total + back
        return total

    level = start
    kept = []
    for _ in range(SUB):
        wet = (level + rain_dt) * soak
        lifted = wet + 0.001
        power = jnp.exp((2.0 / 3.0) * jnp.log(lifted))
        drain = rate * power
        left = jnp.exp(-drain)
        out = wet * (1.0 - left)
        level = land * (wet - out + arrive(out))
        kept.append((wet, lifted, drain, left))
    own = slice(rows, 2 * rows)
    depth_ref[...] = level[own]
    gap = land * (level - observed)
    own_gap = gap[own]
    misfit = jnp.sum(jnp.sum(own_gap * own_gap, axis=1, keepdims=True), axis=0, keepdims=True) * (1.0 / land_total)
    grad = (2.0 / land_total) * land * gap
    g_drain_sum = jnp.zeros_like(grad)
    g_soak_sum = jnp.zeros_like(grad)
    for wet, lifted, drain, left in reversed(kept):
        settled = land * grad
        g_out = collect(settled) - settled
        g_drain = g_out * wet * left * drain
        g_wet = settled + g_out * (1.0 - left) + (2.0 / 3.0) * g_drain / lifted
        g_drain_sum = g_drain_sum + g_drain
        g_soak_sum = g_soak_sum + g_wet * wet
        grad = g_wet * soak
    g_act0 = jnp.where(is_land, -g_drain_sum / manning * (0.27 * sig0 * (1.0 - sig0)), 0.0)[own]
    g_act1 = jnp.where(is_land, -dt * g_soak_sum * sig1, 0.0)[own]
    gact_ref[0] = g_act0
    gact_ref[1] = g_act1
    extra_ref[...] = jnp.zeros_like(extra_ref)
    for j, g in enumerate((g_act0, g_act1)):
        acc = jnp.zeros((hid, cols), jnp.float32)
        for r in range(rows):
            acc = acc + last_ref[:, r * cols:(r + 1) * cols] * g[r:r + 1, :]
        extra_ref[:hid, j:j + 1] = 0.5 * jnp.sum(acc, axis=1, keepdims=True)
        total = jnp.sum(jnp.sum(g, axis=1, keepdims=True), axis=0, keepdims=True)
        extra_ref[hid:hid + 8, j:j + 1] = jnp.broadcast_to(total, (8, 1))
    extra_ref[hid:hid + 8, 2:3] = jnp.broadcast_to(misfit, (8, 1))


def backward_kernel(z_ref, c_ref, w_ref, wback_ref, hwt_ref, gact_ref, extra_ref, grad_ref, gam_scr, gc_scr, acc_scr):
    k = pl.program_id(0)
    steps = pl.num_programs(0)
    rows, cols = gact_ref.shape[1], gact_ref.shape[2]
    hid = c_ref.shape[1]

    @pl.when(k == 0)
    def _():
        acc_scr[...] = jnp.zeros_like(acc_scr)
        gc_scr[...] = jnp.zeros_like(gc_scr)
        for r in range(rows):
            span = slice(r * cols, (r + 1) * cols)
            gam_scr[:, span] = 0.5 * (
                hwt_ref[:, 0:1] * gact_ref[0, r:r + 1, :] + hwt_ref[:, 1:2] * gact_ref[1, r:r + 1, :]
            )

    weight = w_ref[...]
    wback = wback_ref[...]
    for r in range(rows):
        span = slice(r * cols, (r + 1) * cols)
        state = z_ref[0, :, span]
        before = c_ref[0, :, span]
        gates = jnp.tanh(jnp.dot(weight, state, preferred_element_type=jnp.float32))
        t_in = gates[:hid]
        t_keep = gates[hid:2 * hid]
        cand = gates[2 * hid:3 * hid]
        t_out = gates[3 * hid:]
        p_in = t_in + 1.0
        p_keep = t_keep + 1.0
        held = p_keep * before
        fresh = p_in * cand
        squash = jnp.tanh(0.5 * (held + fresh))
        flow = gam_scr[:, span] * (t_out + 1.0)
        grad_c = gc_scr[:, span] + flow * (1.0 - squash * squash)
        e_in = (grad_c * fresh) * (1.0 - t_in)
        e_keep = (grad_c * held) * (1.0 - t_keep)
        e_cand = (grad_c * p_in) * (1.0 - cand * cand)
        e_out = (flow * squash) * (1.0 - t_out)
        gc_scr[:, span] = 0.5 * (grad_c * p_keep)
        low = jnp.concatenate([e_in, e_keep, e_cand, e_out], axis=0).astype(jnp.bfloat16)
        gam_scr[:, span] = jnp.dot(wback, low, preferred_element_type=jnp.float32)
        acc_scr[...] += lax.dot_general(low, state, (((1,), (1,)), ((), ())), preferred_element_type=jnp.float32)

    @pl.when(k == steps - 1)
    def _():
        width = acc_scr.shape[1]
        grad_ref[:, :width] = acc_scr[...]
        grad_ref[:, width:] = extra_ref[...]


def all_sum(value, axis):
    count = lax.axis_size(axis)
    stride = 1
    while stride < count:
        value = value + lax.ppermute(value, axis, [(i, i ^ stride) for i in range(count)])
        stride *= 2
    return value


def neighbours(value):
    count = lax.axis_size("row")
    from_up = lax.ppermute(value, "row", [(i, i + 1) for i in range(count - 1)])
    from_dn = lax.ppermute(value, "row", [(i + 1, i) for i in range(count - 1)])
    return from_up, from_dn


def shards(
    forcing, rainfall, depth_start, observed, land_mask, tile_land, land_rank, flow_code, terrain_slope,
    input_weight, hidden_weight, gate_bias, head_weight, head_offset,
):
    steps, feat, rows, cols = forcing.shape
    hid = hidden_weight.shape[1]
    cells = rows * cols
    depth = feat + hid + PAD
    land_total = LAND_DEV * lax.axis_size("row")
    f32, bf16 = jnp.float32, jnp.bfloat16

    code = jnp.where(land_mask == 1, flow_code + 1, 0).astype(f32)
    fields = jnp.stack([depth_start, rainfall, observed, jnp.sqrt(terrain_slope), code])
    fields_up, fields_dn = neighbours(fields)

    gate = jnp.arange(4 * hid) // hid
    half = jnp.where(gate == 2, 1.0, 0.5)[:, None]
    bias = gate_bias[:, None] * half
    bias_hi = lax.reduce_precision(bias, 8, 7)
    bias_mid = lax.reduce_precision(bias - bias_hi, 8, 7)
    bias_lo = bias - bias_hi - bias_mid
    weight = jnp.concatenate(
        [
            (input_weight.astype(f32) * half).astype(bf16),
            (hidden_weight.astype(f32) * (0.5 * half)).astype(bf16),
            bias_hi.astype(bf16), bias_mid.astype(bf16), bias_lo.astype(bf16),
            jnp.zeros((4 * hid, PAD - 3), bf16),
        ],
        axis=1,
    )
    back_scale = jnp.where(gate < 2, 0.125, 0.25)[:, None]
    wback = (hidden_weight.astype(f32) * back_scale).astype(bf16).T
    hwt = 0.5 * head_weight.T
    place = jnp.arange(feat * rows)
    perm = ((place % feat * rows + place // feat)[:, None] == place[None, :]).astype(bf16)

    whole = lambda *_: (0, 0)
    whole3 = lambda *_: (0, 0, 0)
    z_all, c_all, act, last = pl.pallas_call(
        forward_kernel,
        grid=(steps,),
        in_specs=[
            pl.BlockSpec((1, feat * rows, cols), lambda t: (t, 0, 0)),
            pl.BlockSpec(perm.shape, whole),
            pl.BlockSpec(weight.shape, whole),
            pl.BlockSpec(hwt.shape, whole),
            pl.BlockSpec(memory_space=pltpu.SMEM),
        ],
        out_specs=[
            pl.BlockSpec((1, depth, cells), lambda t: (t, 0, 0)),
            pl.BlockSpec((1, hid, cells), lambda t: (t, 0, 0)),
            pl.BlockSpec((2, rows, cols), whole3),
            pl.BlockSpec((hid, cells), whole),
        ],
        out_shape=[
            jax.ShapeDtypeStruct((steps, depth, cells), bf16),
            jax.ShapeDtypeStruct((steps, hid, cells), f32),
            jax.ShapeDtypeStruct((2, rows, cols), f32),
            jax.ShapeDtypeStruct((hid, cells), f32),
        ],
        scratch_shapes=[pltpu.VMEM((hid, cells), bf16), pltpu.VMEM((hid, cells), f32)],
        compiler_params=pltpu.CompilerParams(vmem_limit_bytes=48 << 20),
    )(forcing.reshape(steps, feat * rows, cols), perm, weight, hwt, head_offset.reshape(1, 2))

    act_up, act_dn = neighbours(act)
    vmem = pl.BlockSpec(memory_space=pltpu.VMEM)

    def water(*refs):
        water_kernel(land_total, *refs)

    depth_final, gact, extra = pl.pallas_call(
        water,
        in_specs=[vmem] * 7,
        out_specs=[vmem] * 3,
        out_shape=[
            jax.ShapeDtypeStruct((rows, cols), f32),
            jax.ShapeDtypeStruct((2, rows, cols), f32),
            jax.ShapeDtypeStruct((4 * hid, EXTRA), f32),
        ],
        compiler_params=pltpu.CompilerParams(vmem_limit_bytes=32 << 20),
    )(fields, fields_up, fields_dn, act, act_up, act_dn, last)

    total_width = depth + EXTRA
    grads = pl.pallas_call(
        backward_kernel,
        grid=(steps,),
        in_specs=[
            pl.BlockSpec((1, depth, cells), lambda k: (steps - 1 - k, 0, 0)),
            pl.BlockSpec((1, hid, cells), lambda k: (steps - 1 - k, 0, 0)),
            pl.BlockSpec(weight.shape, whole),
            pl.BlockSpec(wback.shape, whole),
            pl.BlockSpec(hwt.shape, whole),
            pl.BlockSpec((2, rows, cols), whole3),
            pl.BlockSpec((4 * hid, EXTRA), whole),
        ],
        out_specs=pl.BlockSpec((4 * hid, total_width), whole),
        out_shape=jax.ShapeDtypeStruct((4 * hid, total_width), f32),
        scratch_shapes=[
            pltpu.VMEM((hid, cells), f32),
            pltpu.VMEM((hid, cells), f32),
            pltpu.VMEM((4 * hid, depth), f32),
        ],
        compiler_params=pltpu.CompilerParams(vmem_limit_bytes=48 << 20),
    )(z_all, c_all, weight, wback, hwt, gact, extra)

    total = all_sum(grads, "row")
    true_scale = jnp.where(gate < 2, 0.5, 1.0)[:, None]
    return (
        depth_final,
        total[hid:hid + 1, depth + 2],
        total[:, :feat] * true_scale,
        total[:, feat:feat + hid] * (0.5 * true_scale),
        total[:, feat + hid] * true_scale[:, 0],
        total[:hid, depth:depth + 2].T,
        total[hid, depth:depth + 2],
    )


def solution(mesh):
    return jax.shard_map(
        shards,
        mesh=mesh,
        in_specs=(
            P(None, None, ("groups", "row"), None),
            P(("groups", "row"), None),
            P(("groups", "row"), None),
            P(("groups", "row"), None),
            P("row", None),
            P(),
            P("row", None),
            P("row", None),
            P("row", None),
            P(),
            P(),
            P(),
            P(),
            P(),
        ),
        out_specs=(
            P(("groups", "row"), None),
            P("groups"),
            P("groups", None),
            P("groups", None),
            P("groups"),
            P("groups", None),
            P("groups"),
        ),
        check_vma=False,
    )
```

time: 728 us -> 146 us (0.20)
  other arithmetic: 218 us -> 4.64 us
  local copies, waits for them, and re-layouts: 142 us -> 9.57 us
  Pallas kernels: 0 us -> 92.8 us
  starting transfers between devices: 109 us -> 20.5 us
  matrix products: 80.5 us -> 0 us
  waiting for transfers between devices: 93.9 us -> 17.1 us
  blocking collectives: 63.6 us -> 0 us
  between operations: 16.1 us -> 0.79 us
    pallas_call x0 -> x3, Pallas kernels: none -> 92.8 us  [the longest x1 68.1 us: shards(): pl.pallas_call(backward_kernel, grid=(steps,), in_specs=[pl.BlockSpec((1,...]
    gather x14 -> x0, local copies, waits for them, and re-layouts: 91.4 us -> none  [the longest x2 23 us: shards(): jnp.take(cell_of_order, order_of_slot)]
    dot_general x83 -> x0, matrix products: 80.5 us -> none  [the longest x16 22.6 us: retreat(): lax.dot_general(rounded, state_before, contract_cells, preferred_element_...]
    psum x1 -> x0, blocking collectives: 63.6 us -> none  [shards(): lax.psum((input_part, recur_part, bias_part, head_part, offset_part, misf...]
    dynamic_update_slice x48 -> x0, other arithmetic: 58.6 us -> none  [cell_forward(): final_carry, stash = lax.scan(advance, start_carry, inputs)]
    mul x50 -> x5, other arithmetic: 59.8 us -> 1.48 us  [the longest x1 0.68 us: shards(): hwt = 0.5 * head_weight.T]
    all_to_all x3 -> x0, waiting for transfers between devices: 51.9 us -> none  [the longest x1 45.8 us: shards(): lax.all_to_all(packed, 'row', split_axis=1, concat_axis=1, tiled=True)]
    ppermute x24 -> x8, starting transfers between devices: 68.7 us -> 20.5 us  [the longest x4 10.4 us: all_sum(): lax.ppermute(value, axis, [(i, i ^ stride) for i in range(count)])]
  transfers between devices with their start and end apart: 28 -> 8, of which waited for: 15 -> 5; matrix products, arithmetic and copies ran while one was open for 6% -> 2% of each run, Pallas kernels for 0% -> 16%
where the time goes in v1:
time: 146 us; the launch traced here: 145 us
  Pallas kernels  92.8 us (64%)
  starting transfers between devices  20.5 us (14%)
  waiting for transfers between devices  17.1 us (12%)
  local copies, waits for them, and re-layouts  9.57 us (7%)
  other arithmetic  4.64 us (3%)
    pallas_call x1, Pallas kernels, shards(): pl.pallas_call(backward_kernel, grid=(steps,), in_specs=[pl.BlockSpec((1,...  68.1 us
    pallas_call x1, Pallas kernels, shards(): pl.pallas_call(forward_kernel, grid=(steps,), in_specs=[pl.BlockSpec((1,...  22.9 us
    ppermute x4, waiting for transfers between devices, all_sum(): lax.ppermute(value, axis, [(i, i ^ stride) for i in range(count)])  14 us
    ppermute x4, starting transfers between devices, all_sum(): lax.ppermute(value, axis, [(i, i ^ stride) for i in range(count)])  10.4 us
    unnamed x11, local copies, waits for them, and re-layouts  7.77 us
    ppermute x2, starting transfers between devices, neighbours(): from_up = lax.ppermute(value, 'row', [(i, i + 1) for i in range(count - 1)])  7.5 us
    ppermute x2, waiting for transfers between devices, neighbours(): from_dn = lax.ppermute(value, 'row', [(i + 1, i) for i in range(count - 1)])  3.03 us
  transfers between devices with their start and end apart: 8, of which 5 were waited for; matrix products, arithmetic and copies ran while one was open for 2% of the time, Pallas kernels for 16%

profile of v1, /device:TPU:0, one launch (start us, length us, event | category | flops | bytes accessed | tf_op | source)
XLA Modules:
  0.0 145.4 jit_solution(3404600108494280130)
XLA Ops:
  0.6 0.7 bitcast_dynamic-update-slice_fusion.4
  1.4 0.7 bitcast_dynamic-update-slice_fusion.3
  2.1 0.7 bitcast_dynamic-update-slice_fusion.2
  2.8 0.7 bitcast_dynamic-update-slice_fusion.1
  3.5 0.7 bitcast_dynamic-update-slice_fusion.refs_0_
  4.3 2.3 %collective-permute-start = (f32[5,16,256]{2,1,0:T(8,128)S(1)}, f32[5,16,256]{2,1,0:T(8,128)S(1)}, u32[]{:S(2)}, u32[]{:S(2)}) collective-permute-start(f32[5,16,256]{2,1,0:T(8,128)S(1)} %bitcast_dynamic-update-slice_fusion.refs_0_), channel_id=1, source_target_pairs={{0,1},{1,2},{2,3},{3,4},{4,5},{5,6},{6,7},{7,8},{8,9},{9,10},{10,1... | collective-permute-start | bytes 245768 | tf_op jit(solution)/shard_map/ppermute | solution.py:227
  6.6 1.3 collective-permute-start.1
  8.8 0.7 multiply_convert_fusion
  9.5 0.8 fusion.3
  11.4 2.2 %copy-done = bf16[16,32,16,256]{3,2,1,0:T(8,128)(2,1)S(1)} copy-done((bf16[16,32,16,256]{3,2,1,0:T(8,128)(2,1)S(1)}, bf16[16,32,16,256]{3,2,1,0:T(8,128)(2,1)}, u32[]{:S(2)}) %copy-start) | copy-done | bytes 4194328
  14.2 22.9 %shard_map.171 = (bf16[16,112,4096]{2,1,0:T(8,128)(2,1)}, f32[16,64,4096]{2,1,0:T(8,128)}, f32[2,16,256]{2,1,0:T(8,128)S(1)}, f32[64,4096]{1,0:T(8,128)S(1)}) custom-call(bf16[16,512,256]{2,1,0:T(8,128)(2,1)S(1)} %bitcast.20, bf16[512,512]{1,0:T(8,128)(2,1)S(1)} %fusion.perm_ref, bf16[256,112]{1,0:T(8,128)(2,1)S(1)} %copy.34.w_ref, f32[64,2]{1,0:T(8,128)S(1)} %bitcast.21, ...), custom_call_target="tpu_custom_call" | custom-call | tf_op jit(solution)/shard_map/pallas_call | solution.py:270
  37.1 5.2 %collective-permute-start.2 = (f32[2,16,256]{2,1,0:T(8,128)S(1)}, f32[2,16,256]{2,1,0:T(8,128)S(1)}, u32[]{:S(2)}, u32[]{:S(2)}) collective-permute-start(f32[2,16,256]{2,1,0:T(8,128)S(1)} %get-tuple-element.14.refs_3_), channel_id=1, source_target_pairs={{0,1},{1,2},{2,3},{3,4},{4,5},{5,6},{6,7},{7,8},{8,9},{9,10},{10,1... | collective-permute-start | bytes 98312 | tf_op jit(solution)/shard_map/ppermute | solution.py:227
  42.3 1.3 collective-permute-start.3
  43.6 3.0 %collective-permute-done.3.refs_5_ = f32[2,16,256]{2,1,0:T(8,128)S(1)} collective-permute-done((f32[2,16,256]{2,1,0:T(8,128)S(1)}, f32[2,16,256]{2,1,0:T(8,128)S(1)}, u32[]{:S(2)}, u32[]{:S(2)}) %collective-permute-start.3) | collective-permute-done | bytes 32800 | tf_op jit(solution)/shard_map/ppermute | solution.py:228
  46.6 1.9 %shard_map.172 = (f32[16,256]{1,0:T(8,128)}, f32[2,16,256]{2,1,0:T(8,128)S(1)}, f32[256,16]{1,0:T(8,128)S(1)}) custom-call(f32[5,16,256]{2,1,0:T(8,128)S(1)} %bitcast_dynamic-update-slice_fusion.refs_0_, f32[5,16,256]{2,1,0:T(8,128)S(1)} %collective-permute-done.refs_1_, f32[5,16,256]{2,1,0:T(8,128)S(1)} %collective-permute-done.1.refs_2_, ...), custom_call_target="tpu_custom_call" | custom-call | tf_op jit(solution)/shard_map/pallas_call | solution.py:302
  48.5 68.1 %shard_map.173 = f32[256,128]{1,0:T(8,128)S(1)} custom-call(bf16[16,112,4096]{2,1,0:T(8,128)(2,1)} %get-tuple-element.17.z_ref, f32[16,64,4096]{2,1,0:T(8,128)} %get-tuple-element.18.c_ref, bf16[256,112]{1,0:T(8,128)(2,1)S(1)} %copy.34.w_ref, bf16[64,256]{1,0:T(8,128)(2,1)S(1)} %get-tuple-element.42.wback_ref, f32[64,2]{1,0:T(8,128)S(1)} %bitcast.22, ...), custom_call_target="tpu_custom_call" | custom-call | tf_op jit(solution)/shard_map/pallas_call | solution.py:315
  116.6 2.7 %collective-permute-start.4 = (f32[256,128]{1,0:T(8,128)S(1)}, f32[256,128]{1,0:T(8,128)S(1)}, u32[]{:S(2)}, u32[]{:S(2)}) collective-permute-start(f32[256,128]{1,0:T(8,128)S(1)} %shard_map.173), channel_id=1, source_target_pairs={{0,1},{1,0},{2,3},{3,2},{4,5},{5,4},{6,7},{7,6},{8,9},{9,8},{10,11... | collective-permute-start | bytes 393224 | tf_op jit(solution)/shard_map/ppermute | solution.py:220
  119.3 1.0 collective-permute-done.4
  120.3 3.4 %collective-permute-start.5 = (f32[256,128]{1,0:T(8,128)S(1)}, f32[256,128]{1,0:T(8,128)S(1)}, u32[]{:S(2)}, u32[]{:S(2)}) collective-permute-start(f32[256,128]{1,0:T(8,128)S(1)} %add.57), channel_id=1, source_target_pairs={{0,2},{1,3},{2,0},{3,1},{4,6},{5,7},{6,4},{7,5},{8,10},{9,11},{10,... | collective-permute-start | bytes 393224 | tf_op jit(solution)/shard_map/ppermute | solution.py:220
  123.7 4.0 %collective-permute-done.5 = f32[256,128]{1,0:T(8,128)S(1)} collective-permute-done((f32[256,128]{1,0:T(8,128)S(1)}, f32[256,128]{1,0:T(8,128)S(1)}, u32[]{:S(2)}, u32[]{:S(2)}) %collective-permute-start.5) | collective-permute-done | bytes 131104 | tf_op jit(solution)/shard_map/ppermute | solution.py:220
  127.7 1.6 %collective-permute-start.6 = (f32[256,128]{1,0:T(8,128)S(1)}, f32[256,128]{1,0:T(8,128)S(1)}, u32[]{:S(2)}, u32[]{:S(2)}) collective-permute-start(f32[256,128]{1,0:T(8,128)S(1)} %add.58), channel_id=1, source_target_pairs={{0,4},{1,5},{2,6},{3,7},{4,0},{5,1},{6,2},{7,3},{8,12},{9,13},{10,... | collective-permute-start | bytes 393224 | tf_op jit(solution)/shard_map/ppermute | solution.py:220
  129.4 3.6 %collective-permute-done.6 = f32[256,128]{1,0:T(8,128)S(1)} collective-permute-done((f32[256,128]{1,0:T(8,128)S(1)}, f32[256,128]{1,0:T(8,128)S(1)}, u32[]{:S(2)}, u32[]{:S(2)}) %collective-permute-start.6) | collective-permute-done | bytes 131104 | tf_op jit(solution)/shard_map/ppermute | solution.py:220
  133.0 2.7 %collective-permute-start.7 = (f32[256,128]{1,0:T(8,128)S(1)}, f32[256,128]{1,0:T(8,128)S(1)}, u32[]{:S(2)}, u32[]{:S(2)}) collective-permute-start(f32[256,128]{1,0:T(8,128)S(1)} %add.59), channel_id=1, source_target_pairs={{0,8},{1,9},{2,10},{3,11},{4,12},{5,13},{6,14},{7,15},{8,0},{9,1},... | collective-permute-start | bytes 393224 | tf_op jit(solution)/shard_map/ppermute | solution.py:220
  135.7 5.4 %collective-permute-done.7 = f32[256,128]{1,0:T(8,128)S(1)} collective-permute-done((f32[256,128]{1,0:T(8,128)S(1)}, f32[256,128]{1,0:T(8,128)S(1)}, u32[]{:S(2)}, u32[]{:S(2)}) %collective-permute-start.7) | collective-permute-done | bytes 131104 | tf_op jit(solution)/shard_map/ppermute | solution.py:220
  (35 shorter events, 6.9 us)
Async XLA Ops:
  4.3 42.4 %collective-permute-start = (f32[5,16,256]{2,1,0:T(8,128)S(1)}, f32[5,16,256]{2,1,0:T(8,128)S(1)}, u32[]{:S(2)}, u32[]{:S(2)}) collective-permute-start(f32[5,16,256]{2,1,0:T(8,128)S(1)} %bitcast_dynamic-update-slice_fusion.refs_0_), channel_id=1, source_target_pairs={{0,1},{1,2},{2,3},{3,4},{4,5},{5,6},{6,7},{7,8},{8,9},{9,10},{10,1... | collective-permute-start | bytes 245768 | tf_op jit(solution)/shard_map/ppermute | solution.py:227
  6.6 40.0 %collective-permute-start.1 = (f32[5,16,256]{2,1,0:T(8,128)S(1)}, f32[5,16,256]{2,1,0:T(8,128)S(1)}, u32[]{:S(2)}, u32[]{:S(2)}) collective-permute-start(f32[5,16,256]{2,1,0:T(8,128)S(1)} %bitcast_dynamic-update-slice_fusion.refs_0_), channel_id=1, source_target_pairs={{1,0},{2,1},{3,2},{4,3},{5,4},{6,5},{7,6},{8,7},{9,8},{10,9},{11,1... | collective-permute-start | bytes 245768 | tf_op jit(solution)/shard_map/ppermute | solution.py:228
  11.4 2.2 %copy-start = (bf16[16,32,16,256]{3,2,1,0:T(8,128)(2,1)S(1)}, bf16[16,32,16,256]{3,2,1,0:T(8,128)(2,1)}, u32[]{:S(2)}) copy-start(bf16[16,32,16,256]{3,2,1,0:T(8,128)(2,1)} %param.14) | copy-start | bytes 12582916
  13.6 0.7 copy-start.1
  37.1 6.5 %collective-permute-start.2 = (f32[2,16,256]{2,1,0:T(8,128)S(1)}, f32[2,16,256]{2,1,0:T(8,128)S(1)}, u32[]{:S(2)}, u32[]{:S(2)}) collective-permute-start(f32[2,16,256]{2,1,0:T(8,128)S(1)} %get-tuple-element.14.refs_3_), channel_id=1, source_target_pairs={{0,1},{1,2},{2,3},{3,4},{4,5},{5,6},{6,7},{7,8},{8,9},{9,10},{10,1... | collective-permute-start | bytes 98312 | tf_op jit(solution)/shard_map/ppermute | solution.py:227
  42.3 4.3 %collective-permute-start.3 = (f32[2,16,256]{2,1,0:T(8,128)S(1)}, f32[2,16,256]{2,1,0:T(8,128)S(1)}, u32[]{:S(2)}, u32[]{:S(2)}) collective-permute-start(f32[2,16,256]{2,1,0:T(8,128)S(1)} %get-tuple-element.14.refs_3_), channel_id=1, source_target_pairs={{1,0},{2,1},{3,2},{4,3},{5,4},{6,5},{7,6},{8,7},{9,8},{10,9},{11,1... | collective-permute-start | bytes 98312 | tf_op jit(solution)/shard_map/ppermute | solution.py:228
  116.6 3.7 %collective-permute-start.4 = (f32[256,128]{1,0:T(8,128)S(1)}, f32[256,128]{1,0:T(8,128)S(1)}, u32[]{:S(2)}, u32[]{:S(2)}) collective-permute-start(f32[256,128]{1,0:T(8,128)S(1)} %shard_map.173), channel_id=1, source_target_pairs={{0,1},{1,0},{2,3},{3,2},{4,5},{5,4},{6,7},{7,6},{8,9},{9,8},{10,11... | collective-permute-start | bytes 393224 | tf_op jit(solution)/shard_map/ppermute | solution.py:220
  120.3 7.4 %collective-permute-start.5 = (f32[256,128]{1,0:T(8,128)S(1)}, f32[256,128]{1,0:T(8,128)S(1)}, u32[]{:S(2)}, u32[]{:S(2)}) collective-permute-start(f32[256,128]{1,0:T(8,128)S(1)} %add.57), channel_id=1, source_target_pairs={{0,2},{1,3},{2,0},{3,1},{4,6},{5,7},{6,4},{7,5},{8,10},{9,11},{10,... | collective-permute-start | bytes 393224 | tf_op jit(solution)/shard_map/ppermute | solution.py:220
  127.7 5.3 %collective-permute-start.6 = (f32[256,128]{1,0:T(8,128)S(1)}, f32[256,128]{1,0:T(8,128)S(1)}, u32[]{:S(2)}, u32[]{:S(2)}) collective-permute-start(f32[256,128]{1,0:T(8,128)S(1)} %add.58), channel_id=1, source_target_pairs={{0,4},{1,5},{2,6},{3,7},{4,0},{5,1},{6,2},{7,3},{8,12},{9,13},{10,... | collective-permute-start | bytes 393224 | tf_op jit(solution)/shard_map/ppermute | solution.py:220
  133.0 8.1 %collective-permute-start.7 = (f32[256,128]{1,0:T(8,128)S(1)}, f32[256,128]{1,0:T(8,128)S(1)}, u32[]{:S(2)}, u32[]{:S(2)}) collective-permute-start(f32[256,128]{1,0:T(8,128)S(1)} %add.59), channel_id=1, source_target_pairs={{0,8},{1,9},{2,10},{3,11},{4,12},{5,13},{6,14},{7,15},{8,0},{9,1},... | collective-permute-start | bytes 393224 | tf_op jit(solution)/shard_map/ppermute | solution.py:220

commit v2 on v1

v2 whole, which is shorter than its diff:
```python
import jax
import jax.numpy as jnp
from jax import lax
from jax.experimental import pallas as pl
from jax.experimental.pallas import tpu as pltpu
from jax.sharding import PartitionSpec as P

SUB = 6
LAND_DEV = 2048
PAD = 16
HALO = 2 * SUB
FIELDS = 7
GROUP = 8

compass = ((-1, -1), (-1, 0), (-1, 1), (0, -1), (0, 1), (1, -1), (1, 0), (1, 1))


def gate_rows(array, hid):
    return jnp.concatenate(
        [array[q * hid + g:q * hid + g + GROUP] for g in range(0, hid, GROUP) for q in range(4)], axis=0
    )


def row_scale(shape, hid, values):
    row = lax.broadcasted_iota(jnp.int32, shape, 0) % (4 * GROUP) // GROUP
    return jnp.where(row == 0, values[0], jnp.where(row == 1, values[1], jnp.where(row == 2, values[2], values[3])))


def cell_gates(a, g):
    base = 4 * g
    return [jnp.tanh(a[base + q * GROUP:base + (q + 1) * GROUP]) for q in range(4)]


def forward_kernel(
    x_hbm, input_ref, hidden_ref, bias_ref, head_ref, off_ref, mask_ref, flow_ref, slope_ref, start_ref, rain_ref,
    observed_ref, z_hbm, c_hbm, weight_ref, wback_ref, hwt_ref, own_ref, to_dn_ref, to_up_ref, last_ref,
    x_buf, z_buf, c_buf, perm_scr, x_sem, z_sem, c_sem,
):
    steps = x_buf.shape[0]
    rows, cols = start_ref.shape
    feat = input_ref.shape[1]
    hid = hidden_ref.shape[1]
    cells = rows * cols
    depth = feat + hid + PAD
    f32, bf16 = jnp.float32, jnp.bfloat16

    def x_copy(t):
        return pltpu.make_async_copy(x_hbm.at[t], x_buf.at[t], x_sem.at[t])

    def z_copy(t):
        return pltpu.make_async_copy(z_buf.at[t], z_hbm.at[t], z_sem.at[t])

    def c_copy(t):
        return pltpu.make_async_copy(c_buf.at[t], c_hbm.at[t], c_sem.at[t])

    def span(r):
        return slice(r * cols, (r + 1) * cols)

    for t in range(steps):
        x_copy(t).start()

    shape = perm_scr.shape
    place = lax.broadcasted_iota(jnp.int32, shape, 0)
    source = place % feat * rows + place // feat
    perm_scr[...] = jnp.where(source == lax.broadcasted_iota(jnp.int32, shape, 1), 1.0, 0.0).astype(bf16)
    own_ref[2] = start_ref[...]
    own_ref[3] = rain_ref[...]
    own_ref[4] = observed_ref[...]
    own_ref[5] = jnp.sqrt(slope_ref[...])
    own_ref[6] = jnp.where(mask_ref[...] == 1, flow_ref[...] + 1, 0).astype(f32)
    inputs = gate_rows(input_ref[...].astype(f32), hid)
    hidden = gate_rows(hidden_ref[...].astype(f32), hid)
    bias = jnp.broadcast_to(bias_ref[...], (128, 4 * hid)).T
    bias = gate_rows(bias, hid)
    half = (0.5, 0.5, 1.0, 0.5)
    weight_ref[:, :feat] = (inputs * row_scale(inputs.shape, hid, half)).astype(bf16)
    weight_ref[:, feat:feat + hid] = (0.5 * hidden * row_scale(hidden.shape, hid, half)).astype(bf16)
    bias = bias * row_scale(bias.shape, hid, half)
    bias_hi = bias.astype(bf16).astype(f32)
    bias_mid = (bias - bias_hi).astype(bf16).astype(f32)
    bias_lo = bias - bias_hi - bias_mid
    col_id = lax.broadcasted_iota(jnp.int32, bias.shape, 1)
    bias = jnp.where(col_id == 0, bias_hi, jnp.where(col_id == 1, bias_mid, jnp.where(col_id == 2, bias_lo, 0.0)))
    weight_ref[:, feat + hid:] = bias[:, :PAD].astype(bf16)
    back = hidden * row_scale(hidden.shape, hid, (0.125, 0.125, 0.25, 0.25))
    back = jnp.concatenate([back, jnp.zeros((4 * hid, 128 - hid), f32)], axis=1)
    wback_ref[...] = back.T[:hid].astype(bf16)
    head = jnp.concatenate([head_ref[...], jnp.zeros((126, hid), f32)], axis=0)
    head = jnp.concatenate([head, jnp.zeros((128, 128 - hid), f32)], axis=1)
    hwt_ref[...] = 0.5 * head.T[:hid]

    c_buf[0] = jnp.zeros((hid, cells), f32)
    z_buf[0, feat:feat + hid, :] = jnp.zeros((hid, cells), bf16)
    ones = jnp.where(lax.broadcasted_iota(jnp.int32, (PAD, cells), 0) < 3, 1.0, 0.0).astype(bf16)

    def permute(t):
        x_copy(t).wait()
        moved = jnp.dot(perm_scr[...], x_buf[t], preferred_element_type=f32).astype(bf16)
        for r in range(rows):
            z_buf[t, :feat, span(r)] = moved[r * feat:(r + 1) * feat]
        z_buf[t, feat + hid:, :] = ones

    def step(t, final):
        z_copy(t).start()
        c_copy(t).start()
        weight = weight_ref[...]

        def gates(r):
            return jnp.dot(weight, z_buf[t, :, span(r)], preferred_element_type=f32)

        ahead = gates(0)
        for r in range(rows):
            a = ahead
            ahead = gates(r + 1) if r + 1 < rows else None
            if r == rows // 2 and not final:
                permute(t + 1)
            before = c_buf[t, :, span(r)]
            memories, states = [], []
            for g in range(0, hid, GROUP):
                t_in, t_keep, cand, t_out = cell_gates(a, g)
                memory = 0.5 * ((t_keep + 1.0) * before[g:g + GROUP] + (t_in + 1.0) * cand)
                memories.append(memory)
                states.append((t_out + 1.0) * jnp.tanh(memory))
            state = jnp.concatenate(states, axis=0)
            if final:
                last_ref[:, span(r)] = state
                for j in range(2):
                    act = jnp.sum(state * hwt_ref[:, j:j + 1], axis=0, keepdims=True)
                    own_ref[j, r:r + 1, :] = act + off_ref[j]
            else:
                c_buf[t + 1, :, span(r)] = jnp.concatenate(memories, axis=0)
                z_buf[t + 1, feat:feat + hid, span(r)] = state.astype(bf16)

    permute(0)

    def pair(i, carry):
        step(2 * i, False)
        step(2 * i + 1, False)
        return carry

    lax.fori_loop(0, (steps - 2) // 2, pair, 0)
    step(steps - 2, False)
    step(steps - 1, True)
    for j in range(FIELDS):
        to_dn_ref[j * HALO:(j + 1) * HALO, :] = own_ref[j, rows - HALO:, :]
        to_up_ref[j * HALO:(j + 1) * HALO, :] = own_ref[j, :HALO, :]
    for t in range(steps):
        z_copy(t).wait()
        c_copy(t).wait()


def shift_rows(value, step):
    return pltpu.roll(value, step % value.shape[0], 0)


def shift_cols(value, step, col_id):
    cols = value.shape[1]
    moved = pltpu.roll(value, step % cols, 1)
    edge = 0 if step > 0 else cols - 1
    return jnp.where(col_id == edge, 0.0, moved)


def water_kernel(land_total, own_ref, up_ref, dn_ref, last_ref, depth_ref, gact_ref, extra_ref):
    rows, cols = depth_ref.shape
    hid = last_ref.shape[0]
    spare = jnp.zeros((rows - HALO, cols), jnp.float32)

    def window(j):
        halo = slice(j * HALO, (j + 1) * HALO)
        return jnp.concatenate([spare, up_ref[halo], own_ref[j], dn_ref[halo], spare], axis=0)

    act0, act1, start, rain, observed, root_slope, code = [window(j) for j in range(FIELDS)]
    is_land = code > 0.5
    land = jnp.where(is_land, 1.0, 0.0)
    sig0 = 0.5 * jnp.tanh(0.5 * act0) + 0.5
    sig1 = 0.5 * jnp.tanh(0.5 * act1) + 0.5
    soft1 = jnp.maximum(act1, 0.0) + jnp.log(1.0 + jnp.exp(-jnp.abs(act1)))
    manning = jnp.where(is_land, 0.03 + 0.27 * sig0, 0.1)
    infil = jnp.where(is_land, soft1, 1.0)
    dt = 1.0 / SUB
    col_id = lax.broadcasted_iota(jnp.int32, code.shape, 1)
    masks = [jnp.where(code == float(d + 1), 1.0, 0.0) for d in range(8)]
    soak = land * jnp.exp(-dt * infil)
    rain_dt = dt * rain
    rate = dt * root_slope / manning

    def arrive(out):
        total = None
        for col_step in (-1, 0, 1):
            part = None
            for d, (rs, cs) in enumerate(compass):
                if cs != col_step:
                    continue
                flow = out * masks[d]
                flow = shift_rows(flow, rs) if rs else flow
                part = flow if part is None else part + flow
            part = shift_cols(part, col_step, col_id) if col_step else part
            total = part if total is None else total + part
        return total

    def collect(grad):
        total = None
        for col_step in (-1, 0, 1):
            base = shift_cols(grad, -col_step, col_id) if col_step else grad
            for d, (rs, cs) in enumerate(compass):
                if cs != col_step:
                    continue
                back = shift_rows(base, -rs) if rs else base
                back = back * masks[d]
                total = back if total is None else total + back
        return total

    level = start
    kept = []
    for _ in range(SUB):
        wet = (level + rain_dt) * soak
        lifted = wet + 0.001
        power = jnp.exp((2.0 / 3.0) * jnp.log(lifted))
        drain = rate * power
        left = jnp.exp(-drain)
        out = wet * (1.0 - left)
        level = land * (wet - out + arrive(out))
        kept.append((wet, lifted, drain, left))
    own = slice(rows, 2 * rows)
    depth_ref[...] = level[own]
    gap = land * (level - observed)
    own_gap = gap[own]
    misfit = jnp.sum(jnp.sum(own_gap * own_gap, axis=1, keepdims=True), axis=0, keepdims=True) * (1.0 / land_total)
    grad = (2.0 / land_total) * land * gap
    g_drain_sum = jnp.zeros_like(grad)
    g_soak_sum = jnp.zeros_like(grad)
    for wet, lifted, drain, left in reversed(kept):
        settled = land * grad
        g_out = collect(settled) - settled
        g_drain = g_out * wet * left * drain
        g_wet = settled + g_out * (1.0 - left) + (2.0 / 3.0) * g_drain / lifted
        g_drain_sum = g_drain_sum + g_drain
        g_soak_sum = g_soak_sum + g_wet * wet
        grad = g_wet * soak
    g_act0 = jnp.where(is_land, -g_drain_sum / manning * (0.27 * sig0 * (1.0 - sig0)), 0.0)[own]
    g_act1 = jnp.where(is_land, -dt * g_soak_sum * sig1, 0.0)[own]
    gact_ref[0] = g_act0
    gact_ref[1] = g_act1
    sums, totals = [], []
    for g in (g_act0, g_act1):
        acc = jnp.zeros((hid, cols), jnp.float32)
        for r in range(rows):
            acc = acc + last_ref[:, r * cols:(r + 1) * cols] * g[r:r + 1, :]
        sums.append(acc)
        totals.append(jnp.sum(jnp.sum(g, axis=1, keepdims=True), axis=0, keepdims=True))
    heads = 0.5 * jnp.sum(jnp.concatenate(sums, axis=0).T, axis=0, keepdims=True)
    lane = lax.broadcasted_iota(jnp.int32, heads.shape, 1)
    rest = jnp.where(lane == 0, totals[0], jnp.where(lane == 1, totals[1], jnp.where(lane == 2, misfit, 0.0)))
    line = jnp.concatenate([heads, rest], axis=1)
    row = lax.broadcasted_iota(jnp.int32, extra_ref.shape, 0)
    extra_ref[...] = jnp.where(row == 1, line, 0.0)


def backward_kernel(
    side_ref, z_ref, c_ref, weight_ref, wback_ref, hwt_ref, gact_ref, extra_ref, keep_ref, send_ref, gam_scr, gc_scr, acc_scr
):
    k = pl.program_id(0)
    trips = pl.num_programs(0)
    rows, cols = gact_ref.shape[1], gact_ref.shape[2]
    unroll, hid = c_ref.shape[0], c_ref.shape[1]

    def span(r):
        return slice(r * cols, (r + 1) * cols)

    @pl.when(k == 0)
    def _():
        acc_scr[...] = jnp.zeros_like(acc_scr)
        gc_scr[...] = jnp.zeros_like(gc_scr)
        for r in range(rows):
            gam_scr[:, span(r)] = 0.5 * (
                hwt_ref[:, 0:1] * gact_ref[0, r:r + 1, :] + hwt_ref[:, 1:2] * gact_ref[1, r:r + 1, :]
            )

    weight = weight_ref[...]
    wback = wback_ref[...]
    order = [(u, r) for u in range(unroll - 1, -1, -1) for r in range(rows)]

    def gates(u, r):
        return jnp.dot(weight, z_ref[u, :, span(r)], preferred_element_type=jnp.float32)

    def spread(u, r, low):
        gam_scr[:, span(r)] = jnp.dot(wback, low, preferred_element_type=jnp.float32)
        acc_scr[...] += lax.dot_general(
            z_ref[u, :, span(r)], low, (((1,), (1,)), ((), ())), preferred_element_type=jnp.float32
        )

    ahead = gates(*order[0])
    low = None
    for i, (u, r) in enumerate(order):
        a = ahead
        ahead = gates(*order[i + 1]) if i + 1 < len(order) else None
        if low is not None:
            spread(*order[i - 1], low)
        before = c_ref[u, :, span(r)]
        gam = gam_scr[:, span(r)]
        carried = gc_scr[:, span(r)]
        lows, passed = [], []
        for g in range(0, hid, GROUP):
            part = slice(g, g + GROUP)
            t_in, t_keep, cand, t_out = cell_gates(a, g)
            p_in = t_in + 1.0
            p_keep = t_keep + 1.0
            held = p_keep * before[part]
            fresh = p_in * cand
            squash = jnp.tanh(0.5 * (held + fresh))
            flow = gam[part] * (t_out + 1.0)
            grad_c = carried[part] + flow * (1.0 - squash * squash)
            e_in = (grad_c * fresh) * (1.0 - t_in)
            e_keep = (grad_c * held) * (1.0 - t_keep)
            e_cand = (grad_c * p_in) * (1.0 - cand * cand)
            e_out = (flow * squash) * (1.0 - t_out)
            passed.append(0.5 * (grad_c * p_keep))
            lows.append(jnp.concatenate([e_in, e_keep, e_cand, e_out], axis=0).astype(jnp.bfloat16))
        gc_scr[:, span(r)] = jnp.concatenate(passed, axis=0)
        low = jnp.concatenate(lows, axis=0)
    spread(*order[-1], low)

    @pl.when(k == trips - 1)
    def _():
        used = keep_ref.shape[0] - 8
        whole = jnp.concatenate([acc_scr[:used], extra_ref[...]], axis=0)
        row = lax.broadcasted_iota(jnp.int32, whole.shape, 0)
        whole = jnp.where(row == used, acc_scr[used:used + 1], whole)
        half = whole.shape[1] // 2
        left, right = whole[:, :half], whole[:, half:]
        first = side_ref[0] == 0
        keep_ref[...] = jnp.where(first, left, right)
        send_ref[...] = jnp.where(first, right, left)


def finish_kernel(feat, side_ref, mine_ref, other_ref, input_ref, hidden_ref, bias_ref, head_ref, offset_ref, misfit_ref):
    hid = hidden_ref.shape[1]
    mine, other = mine_ref[...], other_ref[...]
    first = side_ref[0] == 0
    left = jnp.where(first, mine, other)
    right = jnp.where(first, other, mine)
    whole = jnp.concatenate([left, right], axis=1)
    row = feat + hid + 1
    extra = whole[row:row + 1]
    whole = jnp.concatenate([whole, jnp.zeros((128 - whole.shape[0], 4 * hid), jnp.float32)], axis=0)
    turned = whole.T
    turned = turned * row_scale(turned.shape, hid, (0.5, 0.5, 1.0, 1.0))
    turned = jnp.concatenate(
        [turned[4 * g + q * GROUP:4 * g + (q + 1) * GROUP] for q in range(4) for g in range(0, hid, GROUP)], axis=0
    )
    input_ref[...] = turned[:, :feat]
    hidden_ref[...] = 0.5 * turned[:, feat:feat + hid]
    bias_ref[...] = turned.T[feat + hid:feat + hid + 1]
    head_ref[0:1, :] = extra[:, :hid]
    head_ref[1:2, :] = extra[:, hid:2 * hid]
    offset_ref[...] = extra[:, 2 * hid:2 * hid + 2]
    misfit_ref[...] = extra[:, 2 * hid + 2:2 * hid + 3]


def swap(value, stride):
    count = lax.axis_size("row")
    return lax.ppermute(value, "row", [(i, i ^ stride) for i in range(count)])


def shards(
    forcing, rainfall, depth_start, observed, land_mask, tile_land, land_rank, flow_code, terrain_slope,
    input_weight, hidden_weight, gate_bias, head_weight, head_offset,
):
    steps, feat, rows, cols = forcing.shape
    hid = hidden_weight.shape[1]
    cells = rows * cols
    depth = feat + hid + PAD
    payload = feat + hid + 8
    count = lax.axis_size("row")
    land_total = LAND_DEV * count
    f32, bf16 = jnp.float32, jnp.bfloat16
    vmem = pl.BlockSpec(memory_space=pltpu.VMEM)
    smem = pl.BlockSpec(memory_space=pltpu.SMEM)
    hbm = pl.BlockSpec(memory_space=pl.ANY)
    shape = jax.ShapeDtypeStruct

    z_all, c_all, weight, wback, hwt, own, to_dn, to_up, last = pl.pallas_call(
        forward_kernel,
        in_specs=[hbm] + [vmem] * 4 + [smem] + [vmem] * 6,
        out_specs=[hbm] * 2 + [vmem] * 7,
        out_shape=[
            shape((steps, depth, cells), bf16),
            shape((steps, hid, cells), f32),
            shape((4 * hid, depth), bf16),
            shape((hid, 4 * hid), bf16),
            shape((hid, 128), f32),
            shape((FIELDS, rows, cols), f32),
            shape((FIELDS * HALO, cols), f32),
            shape((FIELDS * HALO, cols), f32),
            shape((hid, cells), f32),
        ],
        scratch_shapes=[
            pltpu.VMEM((steps, feat * rows, cols), bf16),
            pltpu.VMEM((steps, depth, cells), bf16),
            pltpu.VMEM((steps, hid, cells), f32),
            pltpu.VMEM((feat * rows, feat * rows), bf16),
            pltpu.SemaphoreType.DMA((steps,)),
            pltpu.SemaphoreType.DMA((steps,)),
            pltpu.SemaphoreType.DMA((steps,)),
        ],
        compiler_params=pltpu.CompilerParams(vmem_limit_bytes=56 << 20),
    )(
        forcing.reshape(steps, feat * rows, cols), input_weight, hidden_weight, gate_bias.reshape(1, 4 * hid),
        head_weight, head_offset, land_mask, flow_code, terrain_slope, depth_start, rainfall, observed,
    )

    from_up = lax.ppermute(to_dn, "row", [(i, i + 1) for i in range(count - 1)])
    from_dn = lax.ppermute(to_up, "row", [(i + 1, i) for i in range(count - 1)])

    def water(*refs):
        water_kernel(land_total, *refs)

    depth_final, gact, extra = pl.pallas_call(
        water,
        in_specs=[vmem] * 4,
        out_specs=[vmem] * 3,
        out_shape=[shape((rows, cols), f32), shape((2, rows, cols), f32), shape((8, 4 * hid), f32)],
        compiler_params=pltpu.CompilerParams(vmem_limit_bytes=32 << 20),
    )(own, from_up, from_dn, last)

    side = (lax.axis_index("row") % 2).astype(jnp.int32).reshape(1)
    unroll = 2
    trips = steps // unroll
    fixed = lambda k: (0, 0)
    keep, send = pl.pallas_call(
        backward_kernel,
        grid=(trips,),
        in_specs=[
            smem,
            pl.BlockSpec((unroll, depth, cells), lambda k: (trips - 1 - k, 0, 0)),
            pl.BlockSpec((unroll, hid, cells), lambda k: (trips - 1 - k, 0, 0)),
            pl.BlockSpec(weight.shape, fixed),
            pl.BlockSpec(wback.shape, fixed),
            pl.BlockSpec(hwt.shape, fixed),
            pl.BlockSpec((2, rows, cols), lambda k: (0, 0, 0)),
            pl.BlockSpec(extra.shape, fixed),
        ],
        out_specs=[pl.BlockSpec((payload, 2 * hid), fixed)] * 2,
        out_shape=[shape((payload, 2 * hid), f32)] * 2,
        scratch_shapes=[
            pltpu.VMEM((hid, cells), f32),
            pltpu.VMEM((hid, cells), f32),
            pltpu.VMEM((depth, 4 * hid), f32),
        ],
        compiler_params=pltpu.CompilerParams(vmem_limit_bytes=56 << 20),
    )(side, z_all, c_all, weight, wback, hwt, gact, extra)

    mine = keep + swap(send, 1)
    stride = 2
    while stride < count:
        mine = mine + swap(mine, stride)
        stride *= 2
    other = swap(mine, 1)

    def finish(*refs):
        finish_kernel(feat, *refs)

    grads = pl.pallas_call(
        finish,
        in_specs=[smem, vmem, vmem],
        out_specs=[vmem] * 6,
        out_shape=[
            shape((4 * hid, feat), f32),
            shape((4 * hid, hid), f32),
            shape((1, 4 * hid), f32),
            shape((2, hid), f32),
            shape((1, 2), f32),
            shape((1, 1), f32),
        ],
    )(side, mine, other)
    return (
        depth_final, grads[5].reshape(1), grads[0], grads[1], grads[2].reshape(4 * hid), grads[3], grads[4].reshape(2),
    )


def solution(mesh):
    return jax.shard_map(
        shards,
        mesh=mesh,
        in_specs=(
            P(None, None, ("groups", "row"), None),
            P(("groups", "row"), None),
            P(("groups", "row"), None),
            P(("groups", "row"), None),
            P("row", None),
            P(),
            P("row", None),
            P("row", None),
            P("row", None),
            P(),
            P(),
            P(),
            P(),
            P(),
        ),
        out_specs=(
            P(("groups", "row"), None),
            P("groups"),
            P("groups", None),
            P("groups", None),
            P("groups"),
            P("groups", None),
            P("groups"),
        ),
        check_vma=False,
    )
```

time: 146 us -> 92.9 us (0.64)
  Pallas kernels: 92.8 us -> 53.3 us
  starting transfers between devices: 20.5 us -> 13.6 us
  other arithmetic: 4.64 us -> 0.85 us
  waiting for transfers between devices: 17.1 us -> 13.9 us
    pallas_call x3 -> x4, Pallas kernels: 92.8 us -> 53.3 us  [the longest x1 29 us: shards(): pl.pallas_call(backward_kernel, grid=(trips,), in_specs=[smem, pl.BlockSp...]
    ppermute x8 -> x7, starting transfers between devices: 20.5 us -> 13.6 us  [the longest x5 9.94 us: swap(): return lax.ppermute(value, 'row', [(i, i ^ stride) for i in range(count)])]
    ppermute x8 -> x7, waiting for transfers between devices: 17.1 us -> 13.9 us  [the longest x5 9.66 us: swap(): return lax.ppermute(value, 'row', [(i, i ^ stride) for i in range(count)])]
    unnamed x11 -> x16, local copies, waits for them, and re-layouts: 7.77 us -> 10.1 us
    convert_element_type x3 -> x0, other arithmetic: 1.57 us -> none  [the longest x1 0.73 us: shards(): (input_weight.astype(f32) * half).astype(bf16)]
    mul x5 -> x0, other arithmetic: 1.48 us -> none  [the longest x1 0.68 us: shards(): hwt = 0.5 * head_weight.T]
  transfers between devices with their start and end apart: 8 -> 7, of which waited for: 5 -> 6; matrix products, arithmetic and copies ran while one was open for 2% -> 0% of each run, Pallas kernels for 16% -> 0%
where the time goes in v2:
time: 92.9 us; the launch traced here: 92.4 us
  Pallas kernels  53.3 us (57%)
  waiting for transfers between devices  13.9 us (15%)
  starting transfers between devices  13.6 us (15%)
  local copies, waits for them, and re-layouts  10.1 us (11%)
    pallas_call x1, Pallas kernels, shards(): pl.pallas_call(backward_kernel, grid=(trips,), in_specs=[smem, pl.BlockSp...  29 us
    pallas_call x1, Pallas kernels, shards(): pl.pallas_call(forward_kernel, in_specs=[hbm] + [vmem] * 4 + [smem] + [vm...  20.6 us
    unnamed x16, local copies, waits for them, and re-layouts  10.1 us
    ppermute x5, starting transfers between devices, swap(): return lax.ppermute(value, 'row', [(i, i ^ stride) for i in range(count)])  9.94 us
    ppermute x5, waiting for transfers between devices, swap(): return lax.ppermute(value, 'row', [(i, i ^ stride) for i in range(count)])  9.66 us
    ppermute x1, waiting for transfers between devices, shards(): from_dn = lax.ppermute(to_up, 'row', [(i + 1, i) for i in range(count - 1)])  4.2 us
    ppermute x1, starting transfers between devices, shards(): from_up = lax.ppermute(to_dn, 'row', [(i, i + 1) for i in range(count - 1)])  2.36 us
    pallas_call x1, Pallas kernels, shards(): pl.pallas_call(water, in_specs=[vmem] * 4, out_specs=[vmem] * 3, out_shap...  1.88 us
  transfers between devices with their start and end apart: 7, of which 6 were waited for; matrix products, arithmetic and copies ran while one was open for 0% of the time, Pallas kernels for 0%

profile of v2, /device:TPU:0, one launch (start us, length us, event | category | flops | bytes accessed | tf_op | source)
XLA Modules:
  0.0 92.4 jit_solution(118738833947038037)
XLA Ops:
  0.6 1.5 %copy.19.input_ref = bf16[256,32]{1,0:T(8,128)(2,1)} copy(bf16[256,32]{0,1:T(8,128)(2,1)} %param.21) | data formatting | bytes 32768 | tf_op args[9]
  2.1 1.5 %copy.20.hidden_ref = bf16[256,64]{1,0:T(8,128)(2,1)} copy(bf16[256,64]{0,1:T(8,128)(2,1)} %param.22) | data formatting | bytes 65536 | tf_op args[10]
  3.6 20.6 %shard_map.171 = (bf16[16,112,4096]{2,1,0:T(8,128)(2,1)}, f32[16,64,4096]{2,1,0:T(8,128)}, bf16[256,112]{1,0:T(8,128)(2,1)}, bf16[64,256]{1,0:T(8,128)(2,1)}, f3...) custom-call(bf16[16,512,256]{2,1,0:T(8,128)(2,1)} %bitcast.6, ...), custom_call_target="tpu_custom_call" | custom-call | tf_op jit(solution)/shard_map/pallas_call | solution.py:382
  24.2 2.4 %collective-permute-start = (f32[84,256]{1,0:T(8,128)}, f32[84,256]{1,0:T(8,128)S(1)}, u32[]{:S(2)}, u32[]{:S(2)}) collective-permute-start(f32[84,256]{1,0:T(8,128)} %get-tuple-element.28), channel_id=1, source_target_pairs={{0,1},{1,2},{2,3},{3,4},{4,5},{5,6},{6,7},{7,8},{8,9},{9,10},{10,1... | collective-permute-start | bytes 258056 | tf_op jit(solution)/shard_map/ppermute | solution.py:412
  26.6 1.3 %collective-permute-start.1 = (f32[84,256]{1,0:T(8,128)}, f32[84,256]{1,0:T(8,128)S(1)}, u32[]{:S(2)}, u32[]{:S(2)}) collective-permute-start(f32[84,256]{1,0:T(8,128)} %get-tuple-element.29), channel_id=1, source_target_pairs={{1,0},{2,1},{3,2},{4,3},{5,4},{6,5},{7,6},{8,7},{9,8},{10,9},{11,1... | collective-permute-start | bytes 258056 | tf_op jit(solution)/shard_map/ppermute | solution.py:413
  27.9 4.2 %collective-permute-done.1.refs_2_ = f32[84,256]{1,0:T(8,128)S(1)} collective-permute-done((f32[84,256]{1,0:T(8,128)}, f32[84,256]{1,0:T(8,128)S(1)}, u32[]{:S(2)}, u32[]{:S(2)}) %collective-permute-start.1) | collective-permute-done | bytes 86048 | tf_op jit(solution)/shard_map/ppermute | solution.py:413
  32.1 1.2 %copy-done = f32[64,4096]{1,0:T(8,128)S(1)} copy-done((f32[64,4096]{1,0:T(8,128)S(1)}, f32[64,4096]{1,0:T(8,128)}, u32[]{:S(2)}) %copy-start) | copy-done | bytes 1048600
  33.3 0.9 copy-done.1
  34.2 1.9 %shard_map.172 = (f32[16,256]{1,0:T(8,128)}, f32[2,16,256]{2,1,0:T(8,128)S(1)}, f32[8,256]{1,0:T(8,128)S(1)}) custom-call(f32[7,16,256]{2,1,0:T(8,128)S(1)} %copy-done.1, f32[84,256]{1,0:T(8,128)S(1)} %collective-permute-done.refs_1_, f32[84,256]{1,0:T(8,128)S(1)} %collective-permute-done.1.refs_2_, f32[64,4096]{1,0:T(8,128)S(1)} %copy-done), custom_call_target="tpu_custom_call" | custom-call | tf_op jit(solution)/shard_map/pallas_call | solution.py:418
  37.3 29.0 %shard_map.173 = (f32[104,128]{1,0:T(8,128)}, f32[104,128]{1,0:T(8,128)}) custom-call(s32[1]{0:T(128)} %bitcast.2.side_ref.refs_0_, bf16[16,112,4096]{2,1,0:T(8,128)(2,1)} %get-tuple-element.32.z_ref, f32[16,64,4096]{2,1,0:T(8,128)} %get-tuple-element.33.c_ref, bf16[256,112]{1,0:T(8,128)(2,1)} %get-tuple-element.34.weight_ref, ...), custom_call_target="tpu_custom_call" | custom-call | tf_op jit(solution)/shard_map/pallas_call | solution.py:430
  66.3 3.2 %collective-permute-start.2 = (f32[104,128]{1,0:T(8,128)}, f32[104,128]{1,0:T(8,128)S(1)}, u32[]{:S(2)}, u32[]{:S(2)}) collective-permute-start(f32[104,128]{1,0:T(8,128)} %get-tuple-element.40), channel_id=1, source_target_pairs={{0,1},{1,0},{2,3},{3,2},{4,5},{5,4},{6,7},{7,6},{8,9},{9,8},{10,11... | collective-permute-start | bytes 159752 | tf_op jit(solution)/shard_map/ppermute | solution.py:362
  69.5 1.1 %collective-permute-done.2 = f32[104,128]{1,0:T(8,128)S(1)} collective-permute-done((f32[104,128]{1,0:T(8,128)}, f32[104,128]{1,0:T(8,128)S(1)}, u32[]{:S(2)}, u32[]{:S(2)}) %collective-permute-start.2) | collective-permute-done | bytes 53280 | tf_op jit(solution)/shard_map/ppermute | solution.py:362
  70.6 0.8 add.17
  71.4 2.4 %collective-permute-start.3 = (f32[104,128]{1,0:T(8,128)S(1)}, f32[104,128]{1,0:T(8,128)S(1)}, u32[]{:S(2)}, u32[]{:S(2)}) collective-permute-start(f32[104,128]{1,0:T(8,128)S(1)} %add.17), channel_id=1, source_target_pairs={{0,2},{1,3},{2,0},{3,1},{4,6},{5,7},{6,4},{7,5},{8,10},{9,11},{10,... | collective-permute-start | bytes 159752 | tf_op jit(solution)/shard_map/ppermute | solution.py:362
  73.8 2.3 %collective-permute-done.3 = f32[104,128]{1,0:T(8,128)S(1)} collective-permute-done((f32[104,128]{1,0:T(8,128)S(1)}, f32[104,128]{1,0:T(8,128)S(1)}, u32[]{:S(2)}, u32[]{:S(2)}) %collective-permute-start.3) | collective-permute-done | bytes 53280 | tf_op jit(solution)/shard_map/ppermute | solution.py:362
  76.2 1.6 %collective-permute-start.4 = (f32[104,128]{1,0:T(8,128)S(1)}, f32[104,128]{1,0:T(8,128)S(1)}, u32[]{:S(2)}, u32[]{:S(2)}) collective-permute-start(f32[104,128]{1,0:T(8,128)S(1)} %add.18), channel_id=1, source_target_pairs={{0,4},{1,5},{2,6},{3,7},{4,0},{5,1},{6,2},{7,3},{8,12},{9,13},{10,... | collective-permute-start | bytes 159752 | tf_op jit(solution)/shard_map/ppermute | solution.py:362
  77.8 2.6 %collective-permute-done.4 = f32[104,128]{1,0:T(8,128)S(1)} collective-permute-done((f32[104,128]{1,0:T(8,128)S(1)}, f32[104,128]{1,0:T(8,128)S(1)}, u32[]{:S(2)}, u32[]{:S(2)}) %collective-permute-start.4) | collective-permute-done | bytes 53280 | tf_op jit(solution)/shard_map/ppermute | solution.py:362
  80.4 2.7 %collective-permute-start.5 = (f32[104,128]{1,0:T(8,128)S(1)}, f32[104,128]{1,0:T(8,128)S(1)}, u32[]{:S(2)}, u32[]{:S(2)}) collective-permute-start(f32[104,128]{1,0:T(8,128)S(1)} %add.19), channel_id=1, source_target_pairs={{0,8},{1,9},{2,10},{3,11},{4,12},{5,13},{6,14},{7,15},{8,0},{9,1},... | collective-permute-start | bytes 159752 | tf_op jit(solution)/shard_map/ppermute | solution.py:362
  83.0 2.4 %collective-permute-done.5 = f32[104,128]{1,0:T(8,128)S(1)} collective-permute-done((f32[104,128]{1,0:T(8,128)S(1)}, f32[104,128]{1,0:T(8,128)S(1)}, u32[]{:S(2)}, u32[]{:S(2)}) %collective-permute-start.5) | collective-permute-done | bytes 53280 | tf_op jit(solution)/shard_map/ppermute | solution.py:362
  85.6 1.2 %collective-permute-done.6.refs_2_ = f32[104,128]{1,0:T(8,128)S(1)} collective-permute-done((f32[104,128]{1,0:T(8,128)S(1)}, f32[104,128]{1,0:T(8,128)S(1)}, u32[]{:S(2)}, u32[]{:S(2)}) %collective-permute-start.6) | collective-permute-done | bytes 53280 | tf_op jit(solution)/shard_map/ppermute | solution.py:362
  86.8 0.6 copy-done.5
  87.4 1.7 %shard_map.174 = (f32[256,32]{1,0:T(8,128)}, f32[256,64]{1,0:T(8,128)}, f32[1,256]{1,0:T(1,128)}, f32[2,64]{1,0:T(2,128)}, f32[1,2]{1,0:T(1,128)}, /*index=5*/f32[1,1]{1,0:T(1,128)}) custom-call(s32[1]{0:T(128)} %bitcast.2.side_ref.refs_0_, f32[104,128]{1,0:T(8,128)} %copy-done.4, f32[104,128]{1,0:T(8,128)} %copy-done.5), custom_call_target="tpu_custom_call" | custom-call | tf_op jit(solution)/shard_map/pallas_call | solution.py:463
  89.2 1.6 %copy.21 = f32[256,32]{0,1:T(8,128)} copy(f32[256,32]{1,0:T(8,128)} %get-tuple-element.49) | data formatting | bytes 65536
  90.8 1.6 %copy.22 = f32[256,64]{0,1:T(8,128)} copy(f32[256,64]{1,0:T(8,128)} %get-tuple-element.50) | data formatting | bytes 131072
  (14 shorter events, 1.3 us)
Async XLA Ops:
  24.2 3.7 %collective-permute-start = (f32[84,256]{1,0:T(8,128)}, f32[84,256]{1,0:T(8,128)S(1)}, u32[]{:S(2)}, u32[]{:S(2)}) collective-permute-start(f32[84,256]{1,0:T(8,128)} %get-tuple-element.28), channel_id=1, source_target_pairs={{0,1},{1,2},{2,3},{3,4},{4,5},{5,6},{6,7},{7,8},{8,9},{9,10},{10,1... | collective-permute-start | bytes 258056 | tf_op jit(solution)/shard_map/ppermute | solution.py:412
  26.6 5.5 %collective-permute-start.1 = (f32[84,256]{1,0:T(8,128)}, f32[84,256]{1,0:T(8,128)S(1)}, u32[]{:S(2)}, u32[]{:S(2)}) collective-permute-start(f32[84,256]{1,0:T(8,128)} %get-tuple-element.29), channel_id=1, source_target_pairs={{1,0},{2,1},{3,2},{4,3},{5,4},{6,5},{7,6},{8,7},{9,8},{10,9},{11,1... | collective-permute-start | bytes 258056 | tf_op jit(solution)/shard_map/ppermute | solution.py:413
  32.1 1.2 %copy-start = (f32[64,4096]{1,0:T(8,128)S(1)}, f32[64,4096]{1,0:T(8,128)}, u32[]{:S(2)}) copy-start(f32[64,4096]{1,0:T(8,128)} %get-tuple-element.30.refs_3_) | copy-start | bytes 3145732
  33.3 0.9 copy-start.1
  36.1 0.6 copy-start.2
  36.7 0.6 copy-start.3
  66.3 4.3 %collective-permute-start.2 = (f32[104,128]{1,0:T(8,128)}, f32[104,128]{1,0:T(8,128)S(1)}, u32[]{:S(2)}, u32[]{:S(2)}) collective-permute-start(f32[104,128]{1,0:T(8,128)} %get-tuple-element.40), channel_id=1, source_target_pairs={{0,1},{1,0},{2,3},{3,2},{4,5},{5,4},{6,7},{7,6},{8,9},{9,8},{10,11... | collective-permute-start | bytes 159752 | tf_op jit(solution)/shard_map/ppermute | solution.py:362
  71.4 4.8 %collective-permute-start.3 = (f32[104,128]{1,0:T(8,128)S(1)}, f32[104,128]{1,0:T(8,128)S(1)}, u32[]{:S(2)}, u32[]{:S(2)}) collective-permute-start(f32[104,128]{1,0:T(8,128)S(1)} %add.17), channel_id=1, source_target_pairs={{0,2},{1,3},{2,0},{3,1},{4,6},{5,7},{6,4},{7,5},{8,10},{9,11},{10,... | collective-permute-start | bytes 159752 | tf_op jit(solution)/shard_map/ppermute | solution.py:362
  76.2 4.2 %collective-permute-start.4 = (f32[104,128]{1,0:T(8,128)S(1)}, f32[104,128]{1,0:T(8,128)S(1)}, u32[]{:S(2)}, u32[]{:S(2)}) collective-permute-start(f32[104,128]{1,0:T(8,128)S(1)} %add.18), channel_id=1, source_target_pairs={{0,4},{1,5},{2,6},{3,7},{4,0},{5,1},{6,2},{7,3},{8,12},{9,13},{10,... | collective-permute-start | bytes 159752 | tf_op jit(solution)/shard_map/ppermute | solution.py:362
  80.4 5.1 %collective-permute-start.5 = (f32[104,128]{1,0:T(8,128)S(1)}, f32[104,128]{1,0:T(8,128)S(1)}, u32[]{:S(2)}, u32[]{:S(2)}) collective-permute-start(f32[104,128]{1,0:T(8,128)S(1)} %add.19), channel_id=1, source_target_pairs={{0,8},{1,9},{2,10},{3,11},{4,12},{5,13},{6,14},{7,15},{8,0},{9,1},... | collective-permute-start | bytes 159752 | tf_op jit(solution)/shard_map/ppermute | solution.py:362
  85.5 1.3 %copy-start.4 = (f32[104,128]{1,0:T(8,128)}, f32[104,128]{1,0:T(8,128)S(1)}, u32[]{:S(2)}) copy-start(f32[104,128]{1,0:T(8,128)S(1)} %add.20.refs_1_) | copy-start | bytes 159748
  85.5 1.3 %collective-permute-start.6 = (f32[104,128]{1,0:T(8,128)S(1)}, f32[104,128]{1,0:T(8,128)S(1)}, u32[]{:S(2)}, u32[]{:S(2)}) collective-permute-start(f32[104,128]{1,0:T(8,128)S(1)} %add.20.refs_1_), channel_id=1, source_target_pairs={{0,1},{1,0},{2,3},{3,2},{4,5},{5,4},{6,7},{7,6},{8,9},{9,8},{10,11... | collective-permute-start | bytes 159752 | tf_op jit(solution)/shard_map/ppermute | solution.py:362
  86.8 0.6 copy-start.5

commit v3 on v2

--- a/solution.py
+++ b/solution.py
@@ -11,6 +11,7 @@
 HALO = 2 * SUB
 FIELDS = 7
 GROUP = 8
+AHEAD = 1
 
 compass = ((-1, -1), (-1, 0), (-1, 1), (0, -1), (0, 1), (1, -1), (1, 0), (1, 1))
 
@@ -38,8 +39,8 @@
 ):
     steps = x_buf.shape[0]
     rows, cols = start_ref.shape
-    feat = input_ref.shape[1]
-    hid = hidden_ref.shape[1]
+    feat = input_ref.shape[0]
+    hid = hidden_ref.shape[0]
     cells = rows * cols
     depth = feat + hid + PAD
     f32, bf16 = jnp.float32, jnp.bfloat16
@@ -56,7 +57,7 @@
     def span(r):
         return slice(r * cols, (r + 1) * cols)
 
-    for t in range(steps):
+    for t in range(2):
         x_copy(t).start()
 
     shape = perm_scr.shape
@@ -68,23 +69,19 @@
     own_ref[4] = observed_ref[...]
     own_ref[5] = jnp.sqrt(slope_ref[...])
     own_ref[6] = jnp.where(mask_ref[...] == 1, flow_ref[...] + 1, 0).astype(f32)
-    inputs = gate_rows(input_ref[...].astype(f32), hid)
-    hidden = gate_rows(hidden_ref[...].astype(f32), hid)
-    bias = jnp.broadcast_to(bias_ref[...], (128, 4 * hid)).T
-    bias = gate_rows(bias, hid)
-    half = (0.5, 0.5, 1.0, 0.5)
-    weight_ref[:, :feat] = (inputs * row_scale(inputs.shape, hid, half)).astype(bf16)
-    weight_ref[:, feat:feat + hid] = (0.5 * hidden * row_scale(hidden.shape, hid, half)).astype(bf16)
-    bias = bias * row_scale(bias.shape, hid, half)
-    bias_hi = bias.astype(bf16).astype(f32)
-    bias_mid = (bias - bias_hi).astype(bf16).astype(f32)
-    bias_lo = bias - bias_hi - bias_mid
-    col_id = lax.broadcasted_iota(jnp.int32, bias.shape, 1)
-    bias = jnp.where(col_id == 0, bias_hi, jnp.where(col_id == 1, bias_mid, jnp.where(col_id == 2, bias_lo, 0.0)))
-    weight_ref[:, feat + hid:] = bias[:, :PAD].astype(bf16)
-    back = hidden * row_scale(hidden.shape, hid, (0.125, 0.125, 0.25, 0.25))
-    back = jnp.concatenate([back, jnp.zeros((4 * hid, 128 - hid), f32)], axis=1)
-    wback_ref[...] = back.T[:hid].astype(bf16)
+    bias = jnp.broadcast_to(bias_ref[...], (128 - feat - hid, 4 * hid))
+    bias = jnp.where(lax.broadcasted_iota(jnp.int32, bias.shape, 0) < 3, bias, 0.0)
+    weight = gate_rows(jnp.concatenate([input_ref[...].astype(f32), hidden_ref[...].astype(f32), bias], axis=0).T, hid)
+    col_id = lax.broadcasted_iota(jnp.int32, weight.shape, 1)
+    back = jnp.where(col_id < feat + hid, weight, 0.0) * row_scale(weight.shape, hid, (0.125, 0.125, 0.25, 0.25))
+    wback_ref[...] = back.T[feat:feat + hid].astype(bf16)
+    weight = weight * row_scale(weight.shape, hid, (0.5, 0.5, 1.0, 0.5))
+    weight = jnp.where((col_id >= feat) & (col_id < feat + hid), 0.5 * weight, weight)
+    high = weight.astype(bf16).astype(f32)
+    middle = (weight - high).astype(bf16).astype(f32)
+    low = weight - high - middle
+    weight = jnp.where(col_id == feat + hid + 1, middle, jnp.where(col_id == feat + hid + 2, low, weight))
+    weight_ref[...] = weight[:, :depth].astype(bf16)
     head = jnp.concatenate([head_ref[...], jnp.zeros((126, hid), f32)], axis=0)
     head = jnp.concatenate([head, jnp.zeros((128, 128 - hid), f32)], axis=1)
     hwt_ref[...] = 0.5 * head.T[:hid]
@@ -95,6 +92,11 @@
 
     def permute(t):
         x_copy(t).wait()
+
+        @pl.when(t + 2 < steps)
+        def _():
+            x_copy(t + 2).start()
+
         moved = jnp.dot(perm_scr[...], x_buf[t], preferred_element_type=f32).astype(bf16)
         for r in range(rows):
             z_buf[t, :feat, span(r)] = moved[r * feat:(r + 1) * feat]
@@ -160,9 +162,8 @@
     return jnp.where(col_id == edge, 0.0, moved)
 
 
-def water_kernel(land_total, own_ref, up_ref, dn_ref, last_ref, depth_ref, gact_ref, extra_ref):
+def water(land_total, own_ref, up_ref, dn_ref, depth_ref):
     rows, cols = depth_ref.shape
-    hid = last_ref.shape[0]
     spare = jnp.zeros((rows - HALO, cols), jnp.float32)
 
     def window(j):
@@ -239,10 +240,15 @@
         grad = g_wet * soak
     g_act0 = jnp.where(is_land, -g_drain_sum / manning * (0.27 * sig0 * (1.0 - sig0)), 0.0)[own]
     g_act1 = jnp.where(is_land, -dt * g_soak_sum * sig1, 0.0)[own]
-    gact_ref[0] = g_act0
-    gact_ref[1] = g_act1
+    return g_act0, g_act1, misfit
+
+
+def head_line(last_ref, gact_ref, misfit):
+    rows, cols = gact_ref.shape[1], gact_ref.shape[2]
+    hid = last_ref.shape[0]
     sums, totals = [], []
-    for g in (g_act0, g_act1):
+    for j in range(2):
+        g = gact_ref[j]
         acc = jnp.zeros((hid, cols), jnp.float32)
         for r in range(rows):
             acc = acc + last_ref[:, r * cols:(r + 1) * cols] * g[r:r + 1, :]
@@ -251,90 +257,122 @@
     heads = 0.5 * jnp.sum(jnp.concatenate(sums, axis=0).T, axis=0, keepdims=True)
     lane = lax.broadcasted_iota(jnp.int32, heads.shape, 1)
     rest = jnp.where(lane == 0, totals[0], jnp.where(lane == 1, totals[1], jnp.where(lane == 2, misfit, 0.0)))
-    line = jnp.concatenate([heads, rest], axis=1)
-    row = lax.broadcasted_iota(jnp.int32, extra_ref.shape, 0)
-    extra_ref[...] = jnp.where(row == 1, line, 0.0)
+    return jnp.concatenate([heads, rest], axis=1)
 
 
 def backward_kernel(
-    side_ref, z_ref, c_ref, weight_ref, wback_ref, hwt_ref, gact_ref, extra_ref, keep_ref, send_ref, gam_scr, gc_scr, acc_scr
+    land_total, unroll, side_ref, z_hbm, c_hbm, weight_hbm, wback_hbm, hwt_hbm, own_hbm, last_hbm, up_ref, dn_ref,
+    depth_ref, keep_ref, send_ref, z_buf, c_buf, weight_ref, wback_ref, hwt_ref, own_ref, last_ref, gact_ref,
+    gam_scr, gc_scr, acc_scr, z_sem, c_sem, small_sem,
 ):
-    k = pl.program_id(0)
-    trips = pl.num_programs(0)
-    rows, cols = gact_ref.shape[1], gact_ref.shape[2]
-    unroll, hid = c_ref.shape[0], c_ref.shape[1]
+    steps, hid = c_buf.shape[0], c_buf.shape[1]
+    rows, cols = depth_ref.shape
 
     def span(r):
         return slice(r * cols, (r + 1) * cols)
 
-    @pl.when(k == 0)
-    def _():
-        acc_scr[...] = jnp.zeros_like(acc_scr)
-        gc_scr[...] = jnp.zeros_like(gc_scr)
-        for r in range(rows):
-            gam_scr[:, span(r)] = 0.5 * (
-                hwt_ref[:, 0:1] * gact_ref[0, r:r + 1, :] + hwt_ref[:, 1:2] * gact_ref[1, r:r + 1, :]
-            )
-
+    def z_copy(t):
+        return pltpu.make_async_copy(z_hbm.at[t], z_buf.at[t], z_sem.at[t])
+
+    def c_copy(t):
+        return pltpu.make_async_copy(c_hbm.at[t], c_buf.at[t], c_sem.at[t])
+
+    pairs = (
+        (own_hbm, own_ref), (hwt_hbm, hwt_ref), (weight_hbm, weight_ref), (wback_hbm, wback_ref), (last_hbm, last_ref),
+    )
+    small = [pltpu.make_async_copy(src, dst, small_sem.at[i]) for i, (src, dst) in enumerate(pairs)]
+    for copy in small[:4]:
+        copy.start()
+    for t in range(steps - 1, steps - 1 - AHEAD * unroll, -1):
+        z_copy(t).start()
+        c_copy(t).start()
+        if t == steps - unroll:
+            small[4].start()
+    acc_scr[...] = jnp.zeros_like(acc_scr)
+    gc_scr[...] = jnp.zeros_like(gc_scr)
+    small[0].wait()
+    g_act0, g_act1, misfit = water(land_total, own_ref, up_ref, dn_ref, depth_ref)
+    gact_ref[0] = g_act0
+    gact_ref[1] = g_act1
+    for copy in small[1:]:
+        copy.wait()
+    for r in range(rows):
+        gam_scr[:, span(r)] = 0.5 * (
+            hwt_ref[:, 0:1] * gact_ref[0, r:r + 1, :] + hwt_ref[:, 1:2] * gact_ref[1, r:r + 1, :]
+        )
+    line = head_line(last_ref, gact_ref, misfit)
     weight = weight_ref[...]
     wback = wback_ref[...]
-    order = [(u, r) for u in range(unroll - 1, -1, -1) for r in range(rows)]
-
-    def gates(u, r):
-        return jnp.dot(weight, z_ref[u, :, span(r)], preferred_element_type=jnp.float32)
-
-    def spread(u, r, low):
+    order = [(u, r) for u in range(unroll) for r in range(rows)]
+
+    def gates(t, r):
+        return jnp.dot(weight, z_buf[t, :, span(r)], preferred_element_type=jnp.float32)
+
+    def spread(t, r, low):
         gam_scr[:, span(r)] = jnp.dot(wback, low, preferred_element_type=jnp.float32)
         acc_scr[...] += lax.dot_general(
-            z_ref[u, :, span(r)], low, (((1,), (1,)), ((), ())), preferred_element_type=jnp.float32
+            z_buf[t, :, span(r)], low, (((1,), (1,)), ((), ())), preferred_element_type=jnp.float32
         )
 
-    ahead = gates(*order[0])
-    low = None
-    for i, (u, r) in enumerate(order):
-        a = ahead
-        ahead = gates(*order[i + 1]) if i + 1 < len(order) else None
-        if low is not None:
-            spread(*order[i - 1], low)
-        before = c_ref[u, :, span(r)]
-        gam = gam_scr[:, span(r)]
-        carried = gc_scr[:, span(r)]
-        lows, passed = [], []
-        for g in range(0, hid, GROUP):
-            part = slice(g, g + GROUP)
-            t_in, t_keep, cand, t_out = cell_gates(a, g)
-            p_in = t_in + 1.0
-            p_keep = t_keep + 1.0
-            held = p_keep * before[part]
-            fresh = p_in * cand
-            squash = jnp.tanh(0.5 * (held + fresh))
-            flow = gam[part] * (t_out + 1.0)
-            grad_c = carried[part] + flow * (1.0 - squash * squash)
-            e_in = (grad_c * fresh) * (1.0 - t_in)
-            e_keep = (grad_c * held) * (1.0 - t_keep)
-            e_cand = (grad_c * p_in) * (1.0 - cand * cand)
-            e_out = (flow * squash) * (1.0 - t_out)
-            passed.append(0.5 * (grad_c * p_keep))
-            lows.append(jnp.concatenate([e_in, e_keep, e_cand, e_out], axis=0).astype(jnp.bfloat16))
-        gc_scr[:, span(r)] = jnp.concatenate(passed, axis=0)
-        low = jnp.concatenate(lows, axis=0)
-    spread(*order[-1], low)
-
-    @pl.when(k == trips - 1)
-    def _():
-        used = keep_ref.shape[0] - 8
-        whole = jnp.concatenate([acc_scr[:used], extra_ref[...]], axis=0)
-        row = lax.broadcasted_iota(jnp.int32, whole.shape, 0)
-        whole = jnp.where(row == used, acc_scr[used:used + 1], whole)
-        half = whole.shape[1] // 2
-        left, right = whole[:, :half], whole[:, half:]
-        first = side_ref[0] == 0
-        keep_ref[...] = jnp.where(first, left, right)
-        send_ref[...] = jnp.where(first, right, left)
+    def hours(k, carry):
+        top = steps - 1 - unroll * k
+        for u in range(unroll):
+            later = top - u - AHEAD * unroll
+
+            @pl.when(later >= 0)
+            def _(later=later):
+                z_copy(later).start()
+                c_copy(later).start()
+
+        for u in range(unroll):
+            z_copy(top - u).wait()
+            c_copy(top - u).wait()
+        ahead = gates(top, 0)
+        low = None
+        for i, (u, r) in enumerate(order):
+            a = ahead
+            ahead = gates(top - order[i + 1][0], order[i + 1][1]) if i + 1 < len(order) else None
+            if low is not None:
+                spread(top - order[i - 1][0], order[i - 1][1], low)
+            before = c_buf[top - u, :, span(r)]
+            gam = gam_scr[:, span(r)]
+            carried = gc_scr[:, span(r)]
+            lows, passed = [], []
+            for g in range(0, hid, GROUP):
+                part = slice(g, g + GROUP)
+                t_in, t_keep, cand, t_out = cell_gates(a, g)
+                p_in = t_in + 1.0
+                p_keep = t_keep + 1.0
+                held = p_keep * before[part]
+                fresh = p_in * cand
+                squash = jnp.tanh(0.5 * (held + fresh))
+                flow = gam[part] * (t_out + 1.0)
+                grad_c = carried[part] + flow * (1.0 - squash * squash)
+                e_in = (grad_c * fresh) * (1.0 - t_in)
+                e_keep = (grad_c * held) * (1.0 - t_keep)
+                e_cand = (grad_c * p_in) * (1.0 - cand * cand)
+                e_out = (flow * squash) * (1.0 - t_out)
+                passed.append(0.5 * (grad_c * p_keep))
+                lows.append(jnp.concatenate([e_in, e_keep, e_cand, e_out], axis=0).astype(jnp.bfloat16))
+            gc_scr[:, span(r)] = jnp.concatenate(passed, axis=0)
+            low = jnp.concatenate(lows, axis=0)
+        spread(top - order[-1][0], order[-1][1], low)
+        return carry
+
+    lax.fori_loop(0, steps // unroll, hours, 0)
+    used = keep_ref.shape[0] - 8
+    row = lax.broadcasted_iota(jnp.int32, (8, 4 * hid), 0)
+    extra = jnp.where(row == 0, acc_scr[used:used + 1], jnp.where(row == 1, line, 0.0))
+    whole = jnp.concatenate([acc_scr[:used], extra], axis=0)
+    half = whole.shape[1] // 2
+    left, right = whole[:, :half], whole[:, half:]
+    first = side_ref[0] == 0
+    keep_ref[...] = jnp.where(first, left, right)
+    send_ref[...] = jnp.where(first, right, left)
 
 
 def finish_kernel(feat, side_ref, mine_ref, other_ref, input_ref, hidden_ref, bias_ref, head_ref, offset_ref, misfit_ref):
-    hid = hidden_ref.shape[1]
+    hid = hidden_ref.shape[0]
     mine, other = mine_ref[...], other_ref[...]
     first = side_ref[0] == 0
     left = jnp.where(first, mine, other)
@@ -348,9 +386,10 @@
     turned = jnp.concatenate(
         [turned[4 * g + q * GROUP:4 * g + (q + 1) * GROUP] for q in range(4) for g in range(0, hid, GROUP)], axis=0
     )
-    input_ref[...] = turned[:, :feat]
-    hidden_ref[...] = 0.5 * turned[:, feat:feat + hid]
-    bias_ref[...] = turned.T[feat + hid:feat + hid + 1]
+    turned = turned.T
+    input_ref[...] = turned[:feat]
+    hidden_ref[...] = 0.5 * turned[feat:feat + hid]
+    bias_ref[...] = turned[feat + hid:feat + hid + 1]
     head_ref[0:1, :] = extra[:, :hid]
     head_ref[1:2, :] = extra[:, hid:2 * hid]
     offset_ref[...] = extra[:, 2 * hid:2 * hid + 2]
@@ -405,50 +444,40 @@
         ],
         compiler_params=pltpu.CompilerParams(vmem_limit_bytes=56 << 20),
     )(
-        forcing.reshape(steps, feat * rows, cols), input_weight, hidden_weight, gate_bias.reshape(1, 4 * hid),
+        forcing.reshape(steps, feat * rows, cols), input_weight.T, hidden_weight.T, gate_bias.reshape(1, 4 * hid),
         head_weight, head_offset, land_mask, flow_code, terrain_slope, depth_start, rainfall, observed,
     )
 
     from_up = lax.ppermute(to_dn, "row", [(i, i + 1) for i in range(count - 1)])
     from_dn = lax.ppermute(to_up, "row", [(i + 1, i) for i in range(count - 1)])
 
-    def water(*refs):
-        water_kernel(land_total, *refs)
-
-    depth_final, gact, extra = pl.pallas_call(
-        water,
-        in_specs=[vmem] * 4,
+    side = (lax.axis_index("row") % 2).astype(jnp.int32).reshape(1)
+    def backward(*refs):
+        backward_kernel(land_total, 2, *refs)
+
+    depth_final, keep, send = pl.pallas_call(
+        backward,
+        in_specs=[smem] + [hbm] * 7 + [vmem] * 2,
         out_specs=[vmem] * 3,
-        out_shape=[shape((rows, cols), f32), shape((2, rows, cols), f32), shape((8, 4 * hid), f32)],
-        compiler_params=pltpu.CompilerParams(vmem_limit_bytes=32 << 20),
-    )(own, from_up, from_dn, last)
-
-    side = (lax.axis_index("row") % 2).astype(jnp.int32).reshape(1)
-    unroll = 2
-    trips = steps // unroll
-    fixed = lambda k: (0, 0)
-    keep, send = pl.pallas_call(
-        backward_kernel,
-        grid=(trips,),
-        in_specs=[
-            smem,
-            pl.BlockSpec((unroll, depth, cells), lambda k: (trips - 1 - k, 0, 0)),
-            pl.BlockSpec((unroll, hid, cells), lambda k: (trips - 1 - k, 0, 0)),
-            pl.BlockSpec(weight.shape, fixed),
-            pl.BlockSpec(wback.shape, fixed),
-            pl.BlockSpec(hwt.shape, fixed),
-            pl.BlockSpec((2, rows, cols), lambda k: (0, 0, 0)),
-            pl.BlockSpec(extra.shape, fixed),
-        ],
-        out_specs=[pl.BlockSpec((payload, 2 * hid), fixed)] * 2,
-        out_shape=[shape((payload, 2 * hid), f32)] * 2,
+        out_shape=[shape((rows, cols), f32), shape((payload, 2 * hid), f32), shape((payload, 2 * hid), f32)],
         scratch_shapes=[
+            pltpu.VMEM((steps, depth, cells), bf16),
+            pltpu.VMEM((steps, hid, cells), f32),
+            pltpu.VMEM((4 * hid, depth), bf16),
+            pltpu.VMEM((hid, 4 * hid), bf16),
+            pltpu.VMEM((hid, 128), f32),
+            pltpu.VMEM((FIELDS, rows, cols), f32),
+            pltpu.VMEM((hid, cells), f32),
+            pltpu.VMEM((2, rows, cols), f32),
             pltpu.VMEM((hid, cells), f32),
             pltpu.VMEM((hid, cells), f32),
             pltpu.VMEM((depth, 4 * hid), f32),
+            pltpu.SemaphoreType.DMA((steps,)),
+            pltpu.SemaphoreType.DMA((steps,)),
+            pltpu.SemaphoreType.DMA((5,)),
         ],
         compiler_params=pltpu.CompilerParams(vmem_limit_bytes=56 << 20),
-    )(side, z_all, c_all, weight, wback, hwt, gact, extra)
+    )(side, z_all, c_all, weight, wback, hwt, own, last, from_up, from_dn)
 
     mine = keep + swap(send, 1)
     stride = 2
@@ -465,8 +494,8 @@
         in_specs=[smem, vmem, vmem],
         out_specs=[vmem] * 6,
         out_shape=[
-            shape((4 * hid, feat), f32),
-            shape((4 * hid, hid), f32),
+            shape((feat, 4 * hid), f32),
+            shape((hid, 4 * hid), f32),
             shape((1, 4 * hid), f32),
             shape((2, hid), f32),
             shape((1, 2), f32),
@@ -474,7 +503,7 @@
         ],
     )(side, mine, other)
     return (
-        depth_final, grads[5].reshape(1), grads[0], grads[1], grads[2].reshape(4 * hid), grads[3], grads[4].reshape(2),
+        depth_final, grads[5].reshape(1), grads[0].T, grads[1].T, grads[2].reshape(4 * hid), grads[3], grads[4].reshape(2),
     )
 
 

time: 92.9 us -> 83.3 us (0.90)
  local copies, waits for them, and re-layouts: 10.1 us -> 1.26 us
    unnamed x16 -> x8, local copies, waits for them, and re-layouts: 10.1 us -> 1.26 us
    pallas_call x2 -> x1, Pallas kernels: 30.9 us -> 30.4 us  [shards(): pl.pallas_call(backward, in_specs=[smem] + [hbm] * 7 + [vmem] * 2, out_sp...]
where the time goes in v3:
time: 83.3 us; the launch traced here: 82.9 us
  Pallas kernels  52.6 us (63%)
  waiting for transfers between devices  13.8 us (17%)
  starting transfers between devices  13.7 us (16%)
  local copies, waits for them, and re-layouts  1.26 us (2%)
  other arithmetic  0.85 us (1%)
    pallas_call x1, Pallas kernels, shards(): pl.pallas_call(backward, in_specs=[smem] + [hbm] * 7 + [vmem] * 2, out_sp...  30.4 us
    pallas_call x1, Pallas kernels, shards(): pl.pallas_call(forward_kernel, in_specs=[hbm] + [vmem] * 4 + [smem] + [vm...  20.5 us
    ppermute x5, starting transfers between devices, swap(): return lax.ppermute(value, 'row', [(i, i ^ stride) for i in range(count)])  10 us
    ppermute x5, waiting for transfers between devices, swap(): return lax.ppermute(value, 'row', [(i, i ^ stride) for i in range(count)])  9.65 us
    ppermute x1, waiting for transfers between devices, shards(): from_dn = lax.ppermute(to_up, 'row', [(i + 1, i) for i in range(count - 1)])  4.18 us
    ppermute x1, starting transfers between devices, shards(): from_up = lax.ppermute(to_dn, 'row', [(i, i + 1) for i in range(count - 1)])  2.38 us
  transfers between devices with their start and end apart: 7, of which 6 were waited for; matrix products, arithmetic and copies ran while one was open for 0% of the time, Pallas kernels for 0%

profile of v3, /device:TPU:0, one launch (start us, length us, event | category | flops | bytes accessed | tf_op | source)
XLA Modules:
  0.0 82.9 jit_solution(5182643000481748721)
XLA Ops:
  0.6 20.5 %shard_map.171 = (bf16[16,112,4096]{2,1,0:T(8,128)(2,1)}, f32[16,64,4096]{2,1,0:T(8,128)}, bf16[256,112]{1,0:T(8,128)(2,1)}, bf16[64,256]{1,0:T(8,128)(2,1)}, f3...) custom-call(bf16[16,512,256]{2,1,0:T(8,128)(2,1)} %bitcast.10, ...), custom_call_target="tpu_custom_call" | custom-call | tf_op jit(solution)/shard_map/pallas_call | solution.py:421
  21.1 2.4 %collective-permute-start = (f32[84,256]{1,0:T(8,128)}, f32[84,256]{1,0:T(8,128)S(1)}, u32[]{:S(2)}, u32[]{:S(2)}) collective-permute-start(f32[84,256]{1,0:T(8,128)} %get-tuple-element.32), channel_id=1, source_target_pairs={{0,1},{1,2},{2,3},{3,4},{4,5},{5,6},{6,7},{7,8},{8,9},{9,10},{10,1... | collective-permute-start | bytes 258056 | tf_op jit(solution)/shard_map/ppermute | solution.py:451
  23.5 1.3 %collective-permute-start.1 = (f32[84,256]{1,0:T(8,128)}, f32[84,256]{1,0:T(8,128)S(1)}, u32[]{:S(2)}, u32[]{:S(2)}) collective-permute-start(f32[84,256]{1,0:T(8,128)} %get-tuple-element.33), channel_id=1, source_target_pairs={{1,0},{2,1},{3,2},{4,3},{5,4},{6,5},{7,6},{8,7},{9,8},{10,9},{11,1... | collective-permute-start | bytes 258056 | tf_op jit(solution)/shard_map/ppermute | solution.py:452
  24.8 0.0 collective-permute-done.refs_8_
  24.8 0.0 copy-start.1
  24.8 4.2 %collective-permute-done.1.refs_9_ = f32[84,256]{1,0:T(8,128)S(1)} collective-permute-done((f32[84,256]{1,0:T(8,128)}, f32[84,256]{1,0:T(8,128)S(1)}, u32[]{:S(2)}, u32[]{:S(2)}) %collective-permute-start.1) | collective-permute-done | bytes 86048 | tf_op jit(solution)/shard_map/ppermute | solution.py:452
  29.0 0.0 copy-done.1
  29.0 0.6 copy-done.2
  29.7 30.4 %shard_map.172 = (f32[16,256]{1,0:T(8,128)}, f32[104,128]{1,0:T(8,128)}, f32[104,128]{1,0:T(8,128)}) custom-call(s32[1]{0:T(128)} %bitcast.refs_0_, bf16[16,112,4096]{2,1,0:T(8,128)(2,1)} %get-tuple-element.25.refs_1_, f32[16,64,4096]{2,1,0:T(8,128)} %get-tuple-element.26.refs_2_, bf16[256,112]{1,0:T(8,128)(2,1)} %get-tuple-element.27.refs_3_, ...), custom_call_target="tpu_custom_call" | custom-call | tf_op jit(solution)/shard_map/pallas_call | solution.py:458
  60.1 3.2 %collective-permute-start.2 = (f32[104,128]{1,0:T(8,128)}, f32[104,128]{1,0:T(8,128)S(1)}, u32[]{:S(2)}, u32[]{:S(2)}) collective-permute-start(f32[104,128]{1,0:T(8,128)} %get-tuple-element.36), channel_id=1, source_target_pairs={{0,1},{1,0},{2,3},{3,2},{4,5},{5,4},{6,7},{7,6},{8,9},{9,8},{10,11... | collective-permute-start | bytes 159752 | tf_op jit(solution)/shard_map/ppermute | solution.py:401
  63.3 1.1 %collective-permute-done.2 = f32[104,128]{1,0:T(8,128)S(1)} collective-permute-done((f32[104,128]{1,0:T(8,128)}, f32[104,128]{1,0:T(8,128)S(1)}, u32[]{:S(2)}, u32[]{:S(2)}) %collective-permute-start.2) | collective-permute-done | bytes 53280 | tf_op jit(solution)/shard_map/ppermute | solution.py:401
  64.4 0.8 add.17
  65.3 2.4 %collective-permute-start.3 = (f32[104,128]{1,0:T(8,128)S(1)}, f32[104,128]{1,0:T(8,128)S(1)}, u32[]{:S(2)}, u32[]{:S(2)}) collective-permute-start(f32[104,128]{1,0:T(8,128)S(1)} %add.17), channel_id=1, source_target_pairs={{0,2},{1,3},{2,0},{3,1},{4,6},{5,7},{6,4},{7,5},{8,10},{9,11},{10,... | collective-permute-start | bytes 159752 | tf_op jit(solution)/shard_map/ppermute | solution.py:401
  67.7 2.3 %collective-permute-done.3 = f32[104,128]{1,0:T(8,128)S(1)} collective-permute-done((f32[104,128]{1,0:T(8,128)S(1)}, f32[104,128]{1,0:T(8,128)S(1)}, u32[]{:S(2)}, u32[]{:S(2)}) %collective-permute-start.3) | collective-permute-done | bytes 53280 | tf_op jit(solution)/shard_map/ppermute | solution.py:401
  70.0 1.6 %collective-permute-start.4 = (f32[104,128]{1,0:T(8,128)S(1)}, f32[104,128]{1,0:T(8,128)S(1)}, u32[]{:S(2)}, u32[]{:S(2)}) collective-permute-start(f32[104,128]{1,0:T(8,128)S(1)} %add.18), channel_id=1, source_target_pairs={{0,4},{1,5},{2,6},{3,7},{4,0},{5,1},{6,2},{7,3},{8,12},{9,13},{10,... | collective-permute-start | bytes 159752 | tf_op jit(solution)/shard_map/ppermute | solution.py:401
  71.7 2.6 %collective-permute-done.4 = f32[104,128]{1,0:T(8,128)S(1)} collective-permute-done((f32[104,128]{1,0:T(8,128)S(1)}, f32[104,128]{1,0:T(8,128)S(1)}, u32[]{:S(2)}, u32[]{:S(2)}) %collective-permute-start.4) | collective-permute-done | bytes 53280 | tf_op jit(solution)/shard_map/ppermute | solution.py:401
  74.2 2.7 %collective-permute-start.5 = (f32[104,128]{1,0:T(8,128)S(1)}, f32[104,128]{1,0:T(8,128)S(1)}, u32[]{:S(2)}, u32[]{:S(2)}) collective-permute-start(f32[104,128]{1,0:T(8,128)S(1)} %add.19), channel_id=1, source_target_pairs={{0,8},{1,9},{2,10},{3,11},{4,12},{5,13},{6,14},{7,15},{8,0},{9,1},... | collective-permute-start | bytes 159752 | tf_op jit(solution)/shard_map/ppermute | solution.py:401
  76.9 2.4 %collective-permute-done.5 = f32[104,128]{1,0:T(8,128)S(1)} collective-permute-done((f32[104,128]{1,0:T(8,128)S(1)}, f32[104,128]{1,0:T(8,128)S(1)}, u32[]{:S(2)}, u32[]{:S(2)}) %collective-permute-start.5) | collective-permute-done | bytes 53280 | tf_op jit(solution)/shard_map/ppermute | solution.py:401
  79.3 0.0 copy-start
  79.4 0.1 collective-permute-start.6
  79.4 1.2 %collective-permute-done.6.refs_2_ = f32[104,128]{1,0:T(8,128)S(1)} collective-permute-done((f32[104,128]{1,0:T(8,128)S(1)}, f32[104,128]{1,0:T(8,128)S(1)}, u32[]{:S(2)}, u32[]{:S(2)}) %collective-permute-start.6) | collective-permute-done | bytes 53280 | tf_op jit(solution)/shard_map/ppermute | solution.py:401
  80.7 0.0 copy-done
  80.7 0.6 copy-done.3
  81.3 1.7 %shard_map.173 = (f32[32,256]{1,0:T(8,128)}, f32[64,256]{1,0:T(8,128)}, f32[1,256]{1,0:T(1,128)}, f32[2,64]{1,0:T(2,128)}, f32[1,2]{1,0:T(1,128)}, /*index=5*/f32[1,1]{1,0:T(1,128)}) custom-call(s32[1]{0:T(128)} %bitcast.refs_0_, f32[104,128]{1,0:T(8,128)} %copy-done, f32[104,128]{1,0:T(8,128)} %copy-done.3), custom_call_target="tpu_custom_call" | custom-call | tf_op jit(solution)/shard_map/pallas_call | solution.py:492
  (5 shorter events, 0.0 us)
Async XLA Ops:
  21.1 3.7 %collective-permute-start = (f32[84,256]{1,0:T(8,128)}, f32[84,256]{1,0:T(8,128)S(1)}, u32[]{:S(2)}, u32[]{:S(2)}) collective-permute-start(f32[84,256]{1,0:T(8,128)} %get-tuple-element.32), channel_id=1, source_target_pairs={{0,1},{1,2},{2,3},{3,4},{4,5},{5,6},{6,7},{7,8},{8,9},{9,10},{10,1... | collective-permute-start | bytes 258056 | tf_op jit(solution)/shard_map/ppermute | solution.py:451
  23.5 5.5 %collective-permute-start.1 = (f32[84,256]{1,0:T(8,128)}, f32[84,256]{1,0:T(8,128)S(1)}, u32[]{:S(2)}, u32[]{:S(2)}) collective-permute-start(f32[84,256]{1,0:T(8,128)} %get-tuple-element.33), channel_id=1, source_target_pairs={{1,0},{2,1},{3,2},{4,3},{5,4},{6,5},{7,6},{8,7},{9,8},{10,9},{11,1... | collective-permute-start | bytes 258056 | tf_op jit(solution)/shard_map/ppermute | solution.py:452
  24.8 4.2 %copy-start.1 = (f32[84,256]{1,0:T(8,128)}, f32[84,256]{1,0:T(8,128)S(1)}, u32[]{:S(2)}) copy-start(f32[84,256]{1,0:T(8,128)S(1)} %collective-permute-done.refs_8_) | copy-start | bytes 258052
  29.0 0.6 copy-start.2
  60.1 4.3 %collective-permute-start.2 = (f32[104,128]{1,0:T(8,128)}, f32[104,128]{1,0:T(8,128)S(1)}, u32[]{:S(2)}, u32[]{:S(2)}) collective-permute-start(f32[104,128]{1,0:T(8,128)} %get-tuple-element.36), channel_id=1, source_target_pairs={{0,1},{1,0},{2,3},{3,2},{4,5},{5,4},{6,7},{7,6},{8,9},{9,8},{10,11... | collective-permute-start | bytes 159752 | tf_op jit(solution)/shard_map/ppermute | solution.py:401
  65.3 4.8 %collective-permute-start.3 = (f32[104,128]{1,0:T(8,128)S(1)}, f32[104,128]{1,0:T(8,128)S(1)}, u32[]{:S(2)}, u32[]{:S(2)}) collective-permute-start(f32[104,128]{1,0:T(8,128)S(1)} %add.17), channel_id=1, source_target_pairs={{0,2},{1,3},{2,0},{3,1},{4,6},{5,7},{6,4},{7,5},{8,10},{9,11},{10,... | collective-permute-start | bytes 159752 | tf_op jit(solution)/shard_map/ppermute | solution.py:401
  70.0 4.2 %collective-permute-start.4 = (f32[104,128]{1,0:T(8,128)S(1)}, f32[104,128]{1,0:T(8,128)S(1)}, u32[]{:S(2)}, u32[]{:S(2)}) collective-permute-start(f32[104,128]{1,0:T(8,128)S(1)} %add.18), channel_id=1, source_target_pairs={{0,4},{1,5},{2,6},{3,7},{4,0},{5,1},{6,2},{7,3},{8,12},{9,13},{10,... | collective-permute-start | bytes 159752 | tf_op jit(solution)/shard_map/ppermute | solution.py:401
  74.2 5.1 %collective-permute-start.5 = (f32[104,128]{1,0:T(8,128)S(1)}, f32[104,128]{1,0:T(8,128)S(1)}, u32[]{:S(2)}, u32[]{:S(2)}) collective-permute-start(f32[104,128]{1,0:T(8,128)S(1)} %add.19), channel_id=1, source_target_pairs={{0,8},{1,9},{2,10},{3,11},{4,12},{5,13},{6,14},{7,15},{8,0},{9,1},... | collective-permute-start | bytes 159752 | tf_op jit(solution)/shard_map/ppermute | solution.py:401
  79.3 1.3 %copy-start = (f32[104,128]{1,0:T(8,128)}, f32[104,128]{1,0:T(8,128)S(1)}, u32[]{:S(2)}) copy-start(f32[104,128]{1,0:T(8,128)S(1)} %add.20.refs_1_) | copy-start | bytes 159748
  79.4 1.3 %collective-permute-start.6 = (f32[104,128]{1,0:T(8,128)S(1)}, f32[104,128]{1,0:T(8,128)S(1)}, u32[]{:S(2)}, u32[]{:S(2)}) collective-permute-start(f32[104,128]{1,0:T(8,128)S(1)} %add.20.refs_1_), channel_id=1, source_target_pairs={{0,1},{1,0},{2,3},{3,2},{4,5},{5,4},{6,7},{7,6},{8,9},{9,8},{10,11... | collective-permute-start | bytes 159752 | tf_op jit(solution)/shard_map/ppermute | solution.py:401
  80.7 0.6 copy-start.3

commit v4 on v3

--- a/solution.py
+++ b/solution.py
@@ -12,6 +12,9 @@
 FIELDS = 7
 GROUP = 8
 AHEAD = 1
+FORWARD_UNROLL = 2
+INS = 10
+OUTS = 7
 
 compass = ((-1, -1), (-1, 0), (-1, 1), (0, -1), (0, 1), (1, -1), (1, 0), (1, 1))
 
@@ -32,11 +35,12 @@
     return [jnp.tanh(a[base + q * GROUP:base + (q + 1) * GROUP]) for q in range(4)]
 
 
-def forward_kernel(
-    x_hbm, input_ref, hidden_ref, bias_ref, head_ref, off_ref, mask_ref, flow_ref, slope_ref, start_ref, rain_ref,
-    observed_ref, z_hbm, c_hbm, weight_ref, wback_ref, hwt_ref, own_ref, to_dn_ref, to_up_ref, last_ref,
-    x_buf, z_buf, c_buf, perm_scr, x_sem, z_sem, c_sem,
-):
+def forward_kernel(x_hbm, off_ref, *refs):
+    in_hbm, (z_hbm, c_hbm), out_hbm = refs[:INS], refs[INS:INS + 2], refs[INS + 2:INS + 2 + OUTS]
+    in_buf, out_buf = refs[INS + 2 + OUTS:2 * INS + 2 + OUTS], refs[2 * INS + 2 + OUTS:2 * INS + 2 + 2 * OUTS]
+    x_buf, z_buf, c_buf, perm_scr, x_sem, z_sem, c_sem, in_sem, out_sem = refs[2 * INS + 2 + 2 * OUTS:]
+    input_ref, hidden_ref, bias_ref, head_ref, mask_ref, flow_ref, slope_ref, start_ref, rain_ref, observed_ref = in_buf
+    weight_ref, wback_ref, hwt_ref, own_ref, to_dn_ref, to_up_ref, last_ref = out_buf
     steps = x_buf.shape[0]
     rows, cols = start_ref.shape
     feat = input_ref.shape[0]
@@ -44,6 +48,10 @@
     cells = rows * cols
     depth = feat + hid + PAD
     f32, bf16 = jnp.float32, jnp.bfloat16
+    ins = [pltpu.make_async_copy(in_hbm[i], in_buf[i], in_sem.at[i]) for i in range(INS)]
+    outs = [pltpu.make_async_copy(out_buf[i], out_hbm[i], out_sem.at[i]) for i in range(OUTS)]
+    for copy in ins:
+        copy.start()
 
     def x_copy(t):
         return pltpu.make_async_copy(x_hbm.at[t], x_buf.at[t], x_sem.at[t])
@@ -57,13 +65,15 @@
     def span(r):
         return slice(r * cols, (r + 1) * cols)
 
-    for t in range(2):
+    for t in range(3):
         x_copy(t).start()
 
     shape = perm_scr.shape
-    place = lax.broadcasted_iota(jnp.int32, shape, 0)
+    place = lax.broadcasted_iota(jnp.int32, (shape[0], 1), 0)
     source = place % feat * rows + place // feat
     perm_scr[...] = jnp.where(source == lax.broadcasted_iota(jnp.int32, shape, 1), 1.0, 0.0).astype(bf16)
+    for copy in ins:
+        copy.wait()
     own_ref[2] = start_ref[...]
     own_ref[3] = rain_ref[...]
     own_ref[4] = observed_ref[...]
@@ -86,25 +96,19 @@
     head = jnp.concatenate([head, jnp.zeros((128, 128 - hid), f32)], axis=1)
     hwt_ref[...] = 0.5 * head.T[:hid]
 
+    for copy in outs[:3]:
+        copy.start()
     c_buf[0] = jnp.zeros((hid, cells), f32)
     z_buf[0, feat:feat + hid, :] = jnp.zeros((hid, cells), bf16)
     ones = jnp.where(lax.broadcasted_iota(jnp.int32, (PAD, cells), 0) < 3, 1.0, 0.0).astype(bf16)
 
     def permute(t):
-        x_copy(t).wait()
-
-        @pl.when(t + 2 < steps)
-        def _():
-            x_copy(t + 2).start()
-
-        moved = jnp.dot(perm_scr[...], x_buf[t], preferred_element_type=f32).astype(bf16)
+        moved = jnp.dot(perm_scr[...], x_buf[jnp.minimum(t, steps - 1)], preferred_element_type=f32).astype(bf16)
         for r in range(rows):
             z_buf[t, :feat, span(r)] = moved[r * feat:(r + 1) * feat]
         z_buf[t, feat + hid:, :] = ones
 
-    def step(t, final):
-        z_copy(t).start()
-        c_copy(t).start()
+    def step(t):
         weight = weight_ref[...]
 
         def gates(r):
@@ -114,7 +118,7 @@
         for r in range(rows):
             a = ahead
             ahead = gates(r + 1) if r + 1 < rows else None
-            if r == rows // 2 and not final:
+            if r == rows // 2:
                 permute(t + 1)
             before = c_buf[t, :, span(r)]
             memories, states = [], []
@@ -124,31 +128,49 @@
                 memories.append(memory)
                 states.append((t_out + 1.0) * jnp.tanh(memory))
             state = jnp.concatenate(states, axis=0)
-            if final:
-                last_ref[:, span(r)] = state
-                for j in range(2):
-                    act = jnp.sum(state * hwt_ref[:, j:j + 1], axis=0, keepdims=True)
-                    own_ref[j, r:r + 1, :] = act + off_ref[j]
-            else:
-                c_buf[t + 1, :, span(r)] = jnp.concatenate(memories, axis=0)
-                z_buf[t + 1, feat:feat + hid, span(r)] = state.astype(bf16)
-
+            last_ref[:, span(r)] = state
+            c_buf[t + 1, :, span(r)] = jnp.concatenate(memories, axis=0)
+            z_buf[t + 1, feat:feat + hid, span(r)] = state.astype(bf16)
+
+    x_copy(0).wait()
     permute(0)
 
-    def pair(i, carry):
-        step(2 * i, False)
-        step(2 * i + 1, False)
+    def trip(i, carry):
+        for u in range(FORWARD_UNROLL):
+            t = FORWARD_UNROLL * i + u
+
+            @pl.when(t + 1 < steps)
+            def _(t=t):
+                x_copy(t + 1).wait()
+
+            @pl.when(t + 3 < steps)
+            def _(t=t):
+                x_copy(t + 3).start()
+
+        for u in range(FORWARD_UNROLL):
+            t = FORWARD_UNROLL * i + u
+            z_copy(t).start()
+            c_copy(t).start()
+            step(t)
         return carry
 
-    lax.fori_loop(0, (steps - 2) // 2, pair, 0)
-    step(steps - 2, False)
-    step(steps - 1, True)
+    lax.fori_loop(0, steps // FORWARD_UNROLL, trip, 0)
+    outs[6].start()
+    for r in range(rows):
+        state = last_ref[:, span(r)]
+        for j in range(2):
+            act = jnp.sum(state * hwt_ref[:, j:j + 1], axis=0, keepdims=True)
+            own_ref[j, r:r + 1, :] = act + off_ref[j]
     for j in range(FIELDS):
         to_dn_ref[j * HALO:(j + 1) * HALO, :] = own_ref[j, rows - HALO:, :]
         to_up_ref[j * HALO:(j + 1) * HALO, :] = own_ref[j, :HALO, :]
+    for copy in outs[3:6]:
+        copy.start()
     for t in range(steps):
         z_copy(t).wait()
         c_copy(t).wait()
+    for copy in outs:
+        copy.wait()
 
 
 def shift_rows(value, step):
@@ -294,13 +316,12 @@
     g_act0, g_act1, misfit = water(land_total, own_ref, up_ref, dn_ref, depth_ref)
     gact_ref[0] = g_act0
     gact_ref[1] = g_act1
-    for copy in small[1:]:
+    for copy in small[1:4]:
         copy.wait()
     for r in range(rows):
         gam_scr[:, span(r)] = 0.5 * (
             hwt_ref[:, 0:1] * gact_ref[0, r:r + 1, :] + hwt_ref[:, 1:2] * gact_ref[1, r:r + 1, :]
         )
-    line = head_line(last_ref, gact_ref, misfit)
     weight = weight_ref[...]
     wback = wback_ref[...]
     order = [(u, r) for u in range(unroll) for r in range(rows)]
@@ -360,6 +381,8 @@
         return carry
 
     lax.fori_loop(0, steps // unroll, hours, 0)
+    small[4].wait()
+    line = head_line(last_ref, gact_ref, misfit)
     used = keep_ref.shape[0] - 8
     row = lax.broadcasted_iota(jnp.int32, (8, 4 * hid), 0)
     extra = jnp.where(row == 0, acc_scr[used:used + 1], jnp.where(row == 1, line, 0.0))
@@ -418,35 +441,38 @@
     hbm = pl.BlockSpec(memory_space=pl.ANY)
     shape = jax.ShapeDtypeStruct
 
+    ins = (
+        input_weight.T, hidden_weight.T, gate_bias.reshape(1, 4 * hid), head_weight,
+        land_mask, flow_code, terrain_slope, depth_start, rainfall, observed,
+    )
+    outs = [
+        shape((4 * hid, depth), bf16),
+        shape((hid, 4 * hid), bf16),
+        shape((hid, 128), f32),
+        shape((FIELDS, rows, cols), f32),
+        shape((FIELDS * HALO, cols), f32),
+        shape((FIELDS * HALO, cols), f32),
+        shape((hid, cells), f32),
+    ]
     z_all, c_all, weight, wback, hwt, own, to_dn, to_up, last = pl.pallas_call(
         forward_kernel,
-        in_specs=[hbm] + [vmem] * 4 + [smem] + [vmem] * 6,
-        out_specs=[hbm] * 2 + [vmem] * 7,
-        out_shape=[
-            shape((steps, depth, cells), bf16),
-            shape((steps, hid, cells), f32),
-            shape((4 * hid, depth), bf16),
-            shape((hid, 4 * hid), bf16),
-            shape((hid, 128), f32),
-            shape((FIELDS, rows, cols), f32),
-            shape((FIELDS * HALO, cols), f32),
-            shape((FIELDS * HALO, cols), f32),
-            shape((hid, cells), f32),
-        ],
-        scratch_shapes=[
+        in_specs=[hbm, smem] + [hbm] * INS,
+        out_specs=[hbm] * (2 + OUTS),
+        out_shape=[shape((steps, depth, cells), bf16), shape((steps, hid, cells), f32)] + outs,
+        scratch_shapes=[pltpu.VMEM(item.shape, item.dtype) for item in (*ins, *outs)]
+        + [
             pltpu.VMEM((steps, feat * rows, cols), bf16),
-            pltpu.VMEM((steps, depth, cells), bf16),
-            pltpu.VMEM((steps, hid, cells), f32),
+            pltpu.VMEM((steps + 1, depth, cells), bf16),
+            pltpu.VMEM((steps + 1, hid, cells), f32),
             pltpu.VMEM((feat * rows, feat * rows), bf16),
             pltpu.SemaphoreType.DMA((steps,)),
             pltpu.SemaphoreType.DMA((steps,)),
             pltpu.SemaphoreType.DMA((steps,)),
+            pltpu.SemaphoreType.DMA((INS,)),
+            pltpu.SemaphoreType.DMA((OUTS,)),
         ],
         compiler_params=pltpu.CompilerParams(vmem_limit_bytes=56 << 20),
-    )(
-        forcing.reshape(steps, feat * rows, cols), input_weight.T, hidden_weight.T, gate_bias.reshape(1, 4 * hid),
-        head_weight, head_offset, land_mask, flow_code, terrain_slope, depth_start, rainfall, observed,
-    )
+    )(forcing.reshape(steps, feat * rows, cols), head_offset, *ins)
 
     from_up = lax.ppermute(to_dn, "row", [(i, i + 1) for i in range(count - 1)])
     from_dn = lax.ppermute(to_up, "row", [(i + 1, i) for i in range(count - 1)])
@@ -501,6 +527,7 @@
             shape((1, 2), f32),
             shape((1, 1), f32),
         ],
+        compiler_params=pltpu.CompilerParams(vmem_limit_bytes=32 << 20),
     )(side, mine, other)
     return (
         depth_final, grads[5].reshape(1), grads[0].T, grads[1].T, grads[2].reshape(4 * hid), grads[3], grads[4].reshape(2),

time: 83.3 us -> 78.2 us (0.939)
  Pallas kernels: 52.6 us -> 48.2 us
    pallas_call x1, Pallas kernels: 20.5 us -> 16.9 us  [shards(): pl.pallas_call(forward_kernel, in_specs=[hbm, smem] + [hbm] * INS, out_sp...]
where the time goes in v4:
time: 78.2 us; the launch traced here: 77.9 us
  Pallas kernels  48.2 us (62%)
  waiting for transfers between devices  13.9 us (18%)
  starting transfers between devices  13.7 us (18%)
  other arithmetic  0.85 us (1%)
    pallas_call x1, Pallas kernels, shards(): pl.pallas_call(backward, in_specs=[smem] + [hbm] * 7 + [vmem] * 2, out_sp...  30.5 us
    pallas_call x1, Pallas kernels, shards(): pl.pallas_call(forward_kernel, in_specs=[hbm, smem] + [hbm] * INS, out_sp...  16.9 us
    ppermute x5, starting transfers between devices, swap(): return lax.ppermute(value, 'row', [(i, i ^ stride) for i in range(count)])  10 us
    ppermute x5, waiting for transfers between devices, swap(): return lax.ppermute(value, 'row', [(i, i ^ stride) for i in range(count)])  9.66 us
    ppermute x1, waiting for transfers between devices, shards(): from_dn = lax.ppermute(to_up, 'row', [(i + 1, i) for i in range(count - 1)])  4.19 us
    ppermute x1, starting transfers between devices, shards(): from_up = lax.ppermute(to_dn, 'row', [(i, i + 1) for i in range(count - 1)])  2.36 us
  transfers between devices with their start and end apart: 7, of which 6 were waited for; matrix products, arithmetic and copies ran while one was open for 0% of the time, Pallas kernels for 0%

profile of v4, /device:TPU:0, one launch (start us, length us, event | category | flops | bytes accessed | tf_op | source)
XLA Modules:
  0.0 77.9 jit_solution(12574859518673588780)
XLA Ops:
  0.6 16.9 %shard_map.171 = (bf16[16,112,4096]{2,1,0:T(8,128)(2,1)}, f32[16,64,4096]{2,1,0:T(8,128)}, bf16[256,112]{1,0:T(8,128)(2,1)}, bf16[64,256]{1,0:T(8,128)(2,1)}, f3...) custom-call(bf16[16,512,256]{2,1,0:T(8,128)(2,1)} %bitcast.10, ...), custom_call_target="tpu_custom_call" | custom-call | tf_op jit(solution)/shard_map/pallas_call | solution.py:457
  17.6 2.4 %collective-permute-start = (f32[84,256]{1,0:T(8,128)}, f32[84,256]{1,0:T(8,128)S(1)}, u32[]{:S(2)}, u32[]{:S(2)}) collective-permute-start(f32[84,256]{1,0:T(8,128)} %get-tuple-element.32), channel_id=1, source_target_pairs={{0,1},{1,2},{2,3},{3,4},{4,5},{5,6},{6,7},{7,8},{8,9},{9,10},{10,1... | collective-permute-start | bytes 258056 | tf_op jit(solution)/shard_map/ppermute | solution.py:477
  19.9 1.3 %collective-permute-start.1 = (f32[84,256]{1,0:T(8,128)}, f32[84,256]{1,0:T(8,128)S(1)}, u32[]{:S(2)}, u32[]{:S(2)}) collective-permute-start(f32[84,256]{1,0:T(8,128)} %get-tuple-element.33), channel_id=1, source_target_pairs={{1,0},{2,1},{3,2},{4,3},{5,4},{6,5},{7,6},{8,7},{9,8},{10,9},{11,1... | collective-permute-start | bytes 258056 | tf_op jit(solution)/shard_map/ppermute | solution.py:478
  21.2 0.0 collective-permute-done.refs_8_
  21.2 0.0 copy-start
  21.3 4.2 %collective-permute-done.1.refs_9_ = f32[84,256]{1,0:T(8,128)S(1)} collective-permute-done((f32[84,256]{1,0:T(8,128)}, f32[84,256]{1,0:T(8,128)S(1)}, u32[]{:S(2)}, u32[]{:S(2)}) %collective-permute-start.1) | collective-permute-done | bytes 86048 | tf_op jit(solution)/shard_map/ppermute | solution.py:478
  25.4 0.0 copy-start.1
  25.4 0.0 copy-done
  25.5 0.6 copy-done.1
  26.1 30.5 %shard_map.172 = (f32[16,256]{1,0:T(8,128)}, f32[104,128]{1,0:T(8,128)}, f32[104,128]{1,0:T(8,128)}) custom-call(s32[1]{0:T(128)} %bitcast.refs_0_, bf16[16,112,4096]{2,1,0:T(8,128)(2,1)} %get-tuple-element.25.refs_1_, f32[16,64,4096]{2,1,0:T(8,128)} %get-tuple-element.26.refs_2_, bf16[256,112]{1,0:T(8,128)(2,1)} %get-tuple-element.27.refs_3_, ...), custom_call_target="tpu_custom_call" | custom-call | tf_op jit(solution)/shard_map/pallas_call | solution.py:484
  56.6 3.2 %collective-permute-start.2 = (f32[104,128]{1,0:T(8,128)}, f32[104,128]{1,0:T(8,128)S(1)}, u32[]{:S(2)}, u32[]{:S(2)}) collective-permute-start(f32[104,128]{1,0:T(8,128)} %get-tuple-element.36), channel_id=1, source_target_pairs={{0,1},{1,0},{2,3},{3,2},{4,5},{5,4},{6,7},{7,6},{8,9},{9,8},{10,11... | collective-permute-start | bytes 159752 | tf_op jit(solution)/shard_map/ppermute | solution.py:424
  59.8 1.1 %collective-permute-done.2 = f32[104,128]{1,0:T(8,128)S(1)} collective-permute-done((f32[104,128]{1,0:T(8,128)}, f32[104,128]{1,0:T(8,128)S(1)}, u32[]{:S(2)}, u32[]{:S(2)}) %collective-permute-start.2) | collective-permute-done | bytes 53280 | tf_op jit(solution)/shard_map/ppermute | solution.py:424
  60.9 0.8 %add.17 = f32[104,128]{1,0:T(8,128)S(1)} add(f32[104,128]{1,0:T(8,128)} %get-tuple-element.35, f32[104,128]{1,0:T(8,128)S(1)} %collective-permute-done.2) | non-fusion elementwise | flops 13312 | bytes 159744 | tf_op jit(solution)/shard_map/add | solution.py:508
  61.7 2.4 %collective-permute-start.3 = (f32[104,128]{1,0:T(8,128)S(1)}, f32[104,128]{1,0:T(8,128)S(1)}, u32[]{:S(2)}, u32[]{:S(2)}) collective-permute-start(f32[104,128]{1,0:T(8,128)S(1)} %add.17), channel_id=1, source_target_pairs={{0,2},{1,3},{2,0},{3,1},{4,6},{5,7},{6,4},{7,5},{8,10},{9,11},{10,... | collective-permute-start | bytes 159752 | tf_op jit(solution)/shard_map/ppermute | solution.py:424
  64.1 2.3 %collective-permute-done.3 = f32[104,128]{1,0:T(8,128)S(1)} collective-permute-done((f32[104,128]{1,0:T(8,128)S(1)}, f32[104,128]{1,0:T(8,128)S(1)}, u32[]{:S(2)}, u32[]{:S(2)}) %collective-permute-start.3) | collective-permute-done | bytes 53280 | tf_op jit(solution)/shard_map/ppermute | solution.py:424
  66.5 1.6 %collective-permute-start.4 = (f32[104,128]{1,0:T(8,128)S(1)}, f32[104,128]{1,0:T(8,128)S(1)}, u32[]{:S(2)}, u32[]{:S(2)}) collective-permute-start(f32[104,128]{1,0:T(8,128)S(1)} %add.18), channel_id=1, source_target_pairs={{0,4},{1,5},{2,6},{3,7},{4,0},{5,1},{6,2},{7,3},{8,12},{9,13},{10,... | collective-permute-start | bytes 159752 | tf_op jit(solution)/shard_map/ppermute | solution.py:424
  68.1 2.6 %collective-permute-done.4 = f32[104,128]{1,0:T(8,128)S(1)} collective-permute-done((f32[104,128]{1,0:T(8,128)S(1)}, f32[104,128]{1,0:T(8,128)S(1)}, u32[]{:S(2)}, u32[]{:S(2)}) %collective-permute-start.4) | collective-permute-done | bytes 53280 | tf_op jit(solution)/shard_map/ppermute | solution.py:424
  70.7 2.7 %collective-permute-start.5 = (f32[104,128]{1,0:T(8,128)S(1)}, f32[104,128]{1,0:T(8,128)S(1)}, u32[]{:S(2)}, u32[]{:S(2)}) collective-permute-start(f32[104,128]{1,0:T(8,128)S(1)} %add.19), channel_id=1, source_target_pairs={{0,8},{1,9},{2,10},{3,11},{4,12},{5,13},{6,14},{7,15},{8,0},{9,1},... | collective-permute-start | bytes 159752 | tf_op jit(solution)/shard_map/ppermute | solution.py:424
  73.3 2.4 %collective-permute-done.5 = f32[104,128]{1,0:T(8,128)S(1)} collective-permute-done((f32[104,128]{1,0:T(8,128)S(1)}, f32[104,128]{1,0:T(8,128)S(1)}, u32[]{:S(2)}, u32[]{:S(2)}) %collective-permute-start.5) | collective-permute-done | bytes 53280 | tf_op jit(solution)/shard_map/ppermute | solution.py:424
  75.8 0.1 collective-permute-start.6
  75.9 1.2 %collective-permute-done.6.refs_2_ = f32[104,128]{1,0:T(8,128)S(1)} collective-permute-done((f32[104,128]{1,0:T(8,128)S(1)}, f32[104,128]{1,0:T(8,128)S(1)}, u32[]{:S(2)}, u32[]{:S(2)}) %collective-permute-start.6) | collective-permute-done | bytes 53280 | tf_op jit(solution)/shard_map/ppermute | solution.py:424
  77.1 0.8 %shard_map.173 = (f32[32,256]{1,0:T(8,128)}, f32[64,256]{1,0:T(8,128)}, f32[1,256]{1,0:T(1,128)}, f32[2,64]{1,0:T(2,128)}, f32[1,2]{1,0:T(1,128)}, /*index=5*/f32[1,1]{1,0:T(1,128)}) custom-call(s32[1]{0:T(128)} %bitcast.refs_0_, f32[104,128]{1,0:T(8,128)S(1)} %add.20.refs_1_, f32[104,128]{1,0:T(8,128)S(1)} %collective-permute-done.6.refs_2_), custom_call_target="tpu_custom_call" | custom-call | tf_op jit(solution)/shard_map/pallas_call | solution.py:518
  (3 shorter events, 0.0 us)
Async XLA Ops:
  17.6 3.7 %collective-permute-start = (f32[84,256]{1,0:T(8,128)}, f32[84,256]{1,0:T(8,128)S(1)}, u32[]{:S(2)}, u32[]{:S(2)}) collective-permute-start(f32[84,256]{1,0:T(8,128)} %get-tuple-element.32), channel_id=1, source_target_pairs={{0,1},{1,2},{2,3},{3,4},{4,5},{5,6},{6,7},{7,8},{8,9},{9,10},{10,1... | collective-permute-start | bytes 258056 | tf_op jit(solution)/shard_map/ppermute | solution.py:477
  19.9 5.5 %collective-permute-start.1 = (f32[84,256]{1,0:T(8,128)}, f32[84,256]{1,0:T(8,128)S(1)}, u32[]{:S(2)}, u32[]{:S(2)}) collective-permute-start(f32[84,256]{1,0:T(8,128)} %get-tuple-element.33), channel_id=1, source_target_pairs={{1,0},{2,1},{3,2},{4,3},{5,4},{6,5},{7,6},{8,7},{9,8},{10,9},{11,1... | collective-permute-start | bytes 258056 | tf_op jit(solution)/shard_map/ppermute | solution.py:478
  21.2 4.2 %copy-start = (f32[84,256]{1,0:T(8,128)}, f32[84,256]{1,0:T(8,128)S(1)}, u32[]{:S(2)}) copy-start(f32[84,256]{1,0:T(8,128)S(1)} %collective-permute-done.refs_8_) | copy-start | bytes 258052
  25.4 0.6 copy-start.1
  56.6 4.3 %collective-permute-start.2 = (f32[104,128]{1,0:T(8,128)}, f32[104,128]{1,0:T(8,128)S(1)}, u32[]{:S(2)}, u32[]{:S(2)}) collective-permute-start(f32[104,128]{1,0:T(8,128)} %get-tuple-element.36), channel_id=1, source_target_pairs={{0,1},{1,0},{2,3},{3,2},{4,5},{5,4},{6,7},{7,6},{8,9},{9,8},{10,11... | collective-permute-start | bytes 159752 | tf_op jit(solution)/shard_map/ppermute | solution.py:424
  61.7 4.8 %collective-permute-start.3 = (f32[104,128]{1,0:T(8,128)S(1)}, f32[104,128]{1,0:T(8,128)S(1)}, u32[]{:S(2)}, u32[]{:S(2)}) collective-permute-start(f32[104,128]{1,0:T(8,128)S(1)} %add.17), channel_id=1, source_target_pairs={{0,2},{1,3},{2,0},{3,1},{4,6},{5,7},{6,4},{7,5},{8,10},{9,11},{10,... | collective-permute-start | bytes 159752 | tf_op jit(solution)/shard_map/ppermute | solution.py:424
  66.5 4.2 %collective-permute-start.4 = (f32[104,128]{1,0:T(8,128)S(1)}, f32[104,128]{1,0:T(8,128)S(1)}, u32[]{:S(2)}, u32[]{:S(2)}) collective-permute-start(f32[104,128]{1,0:T(8,128)S(1)} %add.18), channel_id=1, source_target_pairs={{0,4},{1,5},{2,6},{3,7},{4,0},{5,1},{6,2},{7,3},{8,12},{9,13},{10,... | collective-permute-start | bytes 159752 | tf_op jit(solution)/shard_map/ppermute | solution.py:424
  70.7 5.1 %collective-permute-start.5 = (f32[104,128]{1,0:T(8,128)S(1)}, f32[104,128]{1,0:T(8,128)S(1)}, u32[]{:S(2)}, u32[]{:S(2)}) collective-permute-start(f32[104,128]{1,0:T(8,128)S(1)} %add.19), channel_id=1, source_target_pairs={{0,8},{1,9},{2,10},{3,11},{4,12},{5,13},{6,14},{7,15},{8,0},{9,1},... | collective-permute-start | bytes 159752 | tf_op jit(solution)/shard_map/ppermute | solution.py:424
  75.8 1.3 %collective-permute-start.6 = (f32[104,128]{1,0:T(8,128)S(1)}, f32[104,128]{1,0:T(8,128)S(1)}, u32[]{:S(2)}, u32[]{:S(2)}) collective-permute-start(f32[104,128]{1,0:T(8,128)S(1)} %add.20.refs_1_), channel_id=1, source_target_pairs={{0,1},{1,0},{2,3},{3,2},{4,5},{5,4},{6,7},{7,6},{8,9},{9,8},{10,11... | collective-permute-start | bytes 159752 | tf_op jit(solution)/shard_map/ppermute | solution.py:424

commit v5 on v4

--- a/solution.py
+++ b/solution.py
@@ -283,9 +283,9 @@
 
 
 def backward_kernel(
-    land_total, unroll, side_ref, z_hbm, c_hbm, weight_hbm, wback_hbm, hwt_hbm, own_hbm, last_hbm, up_ref, dn_ref,
-    depth_ref, keep_ref, send_ref, z_buf, c_buf, weight_ref, wback_ref, hwt_ref, own_ref, last_ref, gact_ref,
-    gam_scr, gc_scr, acc_scr, z_sem, c_sem, small_sem,
+    land_total, unroll, side_ref, z_hbm, c_hbm, weight_hbm, wback_hbm, hwt_hbm, own_hbm, last_hbm, up_hbm, dn_hbm,
+    depth_ref, keep_ref, send_ref, z_buf, c_buf, weight_ref, wback_ref, hwt_ref, own_ref, last_ref, up_ref, dn_ref,
+    gact_ref, gam_scr, gc_scr, acc_scr, z_sem, c_sem, small_sem,
 ):
     steps, hid = c_buf.shape[0], c_buf.shape[1]
     rows, cols = depth_ref.shape
@@ -300,23 +300,25 @@
         return pltpu.make_async_copy(c_hbm.at[t], c_buf.at[t], c_sem.at[t])
 
     pairs = (
-        (own_hbm, own_ref), (hwt_hbm, hwt_ref), (weight_hbm, weight_ref), (wback_hbm, wback_ref), (last_hbm, last_ref),
+        (own_hbm, own_ref), (up_hbm, up_ref), (dn_hbm, dn_ref), (hwt_hbm, hwt_ref), (weight_hbm, weight_ref),
+        (wback_hbm, wback_ref), (last_hbm, last_ref),
     )
     small = [pltpu.make_async_copy(src, dst, small_sem.at[i]) for i, (src, dst) in enumerate(pairs)]
-    for copy in small[:4]:
+    for copy in small[:6]:
         copy.start()
     for t in range(steps - 1, steps - 1 - AHEAD * unroll, -1):
         z_copy(t).start()
         c_copy(t).start()
         if t == steps - unroll:
-            small[4].start()
+            small[6].start()
     acc_scr[...] = jnp.zeros_like(acc_scr)
     gc_scr[...] = jnp.zeros_like(gc_scr)
-    small[0].wait()
+    for copy in small[:3]:
+        copy.wait()
     g_act0, g_act1, misfit = water(land_total, own_ref, up_ref, dn_ref, depth_ref)
     gact_ref[0] = g_act0
     gact_ref[1] = g_act1
-    for copy in small[1:4]:
+    for copy in small[3:6]:
         copy.wait()
     for r in range(rows):
         gam_scr[:, span(r)] = 0.5 * (
@@ -353,8 +355,6 @@
         for i, (u, r) in enumerate(order):
             a = ahead
             ahead = gates(top - order[i + 1][0], order[i + 1][1]) if i + 1 < len(order) else None
-            if low is not None:
-                spread(top - order[i - 1][0], order[i - 1][1], low)
             before = c_buf[top - u, :, span(r)]
             gam = gam_scr[:, span(r)]
             carried = gc_scr[:, span(r)]
@@ -376,12 +376,14 @@
                 passed.append(0.5 * (grad_c * p_keep))
                 lows.append(jnp.concatenate([e_in, e_keep, e_cand, e_out], axis=0).astype(jnp.bfloat16))
             gc_scr[:, span(r)] = jnp.concatenate(passed, axis=0)
+            if low is not None:
+                spread(top - order[i - 1][0], order[i - 1][1], low)
             low = jnp.concatenate(lows, axis=0)
         spread(top - order[-1][0], order[-1][1], low)
         return carry
 
     lax.fori_loop(0, steps // unroll, hours, 0)
-    small[4].wait()
+    small[6].wait()
     line = head_line(last_ref, gact_ref, misfit)
     used = keep_ref.shape[0] - 8
     row = lax.broadcasted_iota(jnp.int32, (8, 4 * hid), 0)
@@ -483,7 +485,7 @@
 
     depth_final, keep, send = pl.pallas_call(
         backward,
-        in_specs=[smem] + [hbm] * 7 + [vmem] * 2,
+        in_specs=[smem] + [hbm] * 9,
         out_specs=[vmem] * 3,
         out_shape=[shape((rows, cols), f32), shape((payload, 2 * hid), f32), shape((payload, 2 * hid), f32)],
         scratch_shapes=[
@@ -494,13 +496,15 @@
             pltpu.VMEM((hid, 128), f32),
             pltpu.VMEM((FIELDS, rows, cols), f32),
             pltpu.VMEM((hid, cells), f32),
+            pltpu.VMEM((FIELDS * HALO, cols), f32),
+            pltpu.VMEM((FIELDS * HALO, cols), f32),
             pltpu.VMEM((2, rows, cols), f32),
             pltpu.VMEM((hid, cells), f32),
             pltpu.VMEM((hid, cells), f32),
             pltpu.VMEM((depth, 4 * hid), f32),
             pltpu.SemaphoreType.DMA((steps,)),
             pltpu.SemaphoreType.DMA((steps,)),
-            pltpu.SemaphoreType.DMA((5,)),
+            pltpu.SemaphoreType.DMA((7,)),
         ],
         compiler_params=pltpu.CompilerParams(vmem_limit_bytes=56 << 20),
     )(side, z_all, c_all, weight, wback, hwt, own, last, from_up, from_dn)

time: 78.2 us -> 77.4 us (0.990)
  Pallas kernels: 48.2 us -> 47.4 us
    pallas_call x1, Pallas kernels: 30.5 us -> 29.6 us  [shards(): pl.pallas_call(backward, in_specs=[smem] + [hbm] * 9, out_specs=[vmem] *...]
where the time goes in v5:
time: 77.4 us; the launch traced here: 77.1 us
  Pallas kernels  47.4 us (61%)
  waiting for transfers between devices  13.9 us (18%)
  starting transfers between devices  13.7 us (18%)
  other arithmetic  0.85 us (1%)
    pallas_call x1, Pallas kernels, shards(): pl.pallas_call(backward, in_specs=[smem] + [hbm] * 9, out_specs=[vmem] *...  29.6 us
    pallas_call x1, Pallas kernels, shards(): pl.pallas_call(forward_kernel, in_specs=[hbm, smem] + [hbm] * INS, out_sp...  16.9 us
    ppermute x5, starting transfers between devices, swap(): return lax.ppermute(value, 'row', [(i, i ^ stride) for i in range(count)])  10 us
    ppermute x5, waiting for transfers between devices, swap(): return lax.ppermute(value, 'row', [(i, i ^ stride) for i in range(count)])  9.66 us
    ppermute x1, waiting for transfers between devices, shards(): from_dn = lax.ppermute(to_up, 'row', [(i + 1, i) for i in range(count - 1)])  4.19 us
    ppermute x1, starting transfers between devices, shards(): from_up = lax.ppermute(to_dn, 'row', [(i, i + 1) for i in range(count - 1)])  2.36 us
  transfers between devices with their start and end apart: 7, of which 6 were waited for; matrix products, arithmetic and copies ran while one was open for 0% of the time, Pallas kernels for 0%

profile of v5, /device:TPU:0, one launch (start us, length us, event | category | flops | bytes accessed | tf_op | source)
XLA Modules:
  0.0 77.1 jit_solution(11803031965969171827)
XLA Ops:
  0.6 16.9 %shard_map.171 = (bf16[16,112,4096]{2,1,0:T(8,128)(2,1)}, f32[16,64,4096]{2,1,0:T(8,128)}, bf16[256,112]{1,0:T(8,128)(2,1)}, bf16[64,256]{1,0:T(8,128)(2,1)}, f3...) custom-call(bf16[16,512,256]{2,1,0:T(8,128)(2,1)} %bitcast.10, ...), custom_call_target="tpu_custom_call" | custom-call | tf_op jit(solution)/shard_map/pallas_call | solution.py:459
  17.6 2.4 %collective-permute-start = (f32[84,256]{1,0:T(8,128)}, f32[84,256]{1,0:T(8,128)S(1)}, u32[]{:S(2)}, u32[]{:S(2)}) collective-permute-start(f32[84,256]{1,0:T(8,128)} %get-tuple-element.32), channel_id=1, source_target_pairs={{0,1},{1,2},{2,3},{3,4},{4,5},{5,6},{6,7},{7,8},{8,9},{9,10},{10,1... | collective-permute-start | bytes 258056 | tf_op jit(solution)/shard_map/ppermute | solution.py:479
  19.9 1.3 %collective-permute-start.1 = (f32[84,256]{1,0:T(8,128)}, f32[84,256]{1,0:T(8,128)S(1)}, u32[]{:S(2)}, u32[]{:S(2)}) collective-permute-start(f32[84,256]{1,0:T(8,128)} %get-tuple-element.33), channel_id=1, source_target_pairs={{1,0},{2,1},{3,2},{4,3},{5,4},{6,5},{7,6},{8,7},{9,8},{10,9},{11,1... | collective-permute-start | bytes 258056 | tf_op jit(solution)/shard_map/ppermute | solution.py:480
  21.2 0.0 collective-permute-done.refs_8_
  21.2 0.0 copy-start
  21.3 4.2 %collective-permute-done.1.refs_9_ = f32[84,256]{1,0:T(8,128)S(1)} collective-permute-done((f32[84,256]{1,0:T(8,128)}, f32[84,256]{1,0:T(8,128)S(1)}, u32[]{:S(2)}, u32[]{:S(2)}) %collective-permute-start.1) | collective-permute-done | bytes 86048 | tf_op jit(solution)/shard_map/ppermute | solution.py:480
  25.4 0.0 copy-start.1
  25.4 0.0 copy-done
  25.5 0.6 copy-done.1
  26.1 29.6 %shard_map.172 = (f32[16,256]{1,0:T(8,128)}, f32[104,128]{1,0:T(8,128)}, f32[104,128]{1,0:T(8,128)}) custom-call(s32[1]{0:T(128)} %bitcast.refs_0_, bf16[16,112,4096]{2,1,0:T(8,128)(2,1)} %get-tuple-element.25.refs_1_, f32[16,64,4096]{2,1,0:T(8,128)} %get-tuple-element.26.refs_2_, bf16[256,112]{1,0:T(8,128)(2,1)} %get-tuple-element.27.refs_3_, ...), custom_call_target="tpu_custom_call" | custom-call | tf_op jit(solution)/shard_map/pallas_call | solution.py:486
  55.7 3.2 %collective-permute-start.2 = (f32[104,128]{1,0:T(8,128)}, f32[104,128]{1,0:T(8,128)S(1)}, u32[]{:S(2)}, u32[]{:S(2)}) collective-permute-start(f32[104,128]{1,0:T(8,128)} %get-tuple-element.36), channel_id=1, source_target_pairs={{0,1},{1,0},{2,3},{3,2},{4,5},{5,4},{6,7},{7,6},{8,9},{9,8},{10,11... | collective-permute-start | bytes 159752 | tf_op jit(solution)/shard_map/ppermute | solution.py:426
  59.0 1.1 %collective-permute-done.2 = f32[104,128]{1,0:T(8,128)S(1)} collective-permute-done((f32[104,128]{1,0:T(8,128)}, f32[104,128]{1,0:T(8,128)S(1)}, u32[]{:S(2)}, u32[]{:S(2)}) %collective-permute-start.2) | collective-permute-done | bytes 53280 | tf_op jit(solution)/shard_map/ppermute | solution.py:426
  60.1 0.8 %add.17 = f32[104,128]{1,0:T(8,128)S(1)} add(f32[104,128]{1,0:T(8,128)} %get-tuple-element.35, f32[104,128]{1,0:T(8,128)S(1)} %collective-permute-done.2) | non-fusion elementwise | flops 13312 | bytes 159744 | tf_op jit(solution)/shard_map/add | solution.py:512
  60.9 2.4 %collective-permute-start.3 = (f32[104,128]{1,0:T(8,128)S(1)}, f32[104,128]{1,0:T(8,128)S(1)}, u32[]{:S(2)}, u32[]{:S(2)}) collective-permute-start(f32[104,128]{1,0:T(8,128)S(1)} %add.17), channel_id=1, source_target_pairs={{0,2},{1,3},{2,0},{3,1},{4,6},{5,7},{6,4},{7,5},{8,10},{9,11},{10,... | collective-permute-start | bytes 159752 | tf_op jit(solution)/shard_map/ppermute | solution.py:426
  63.3 2.3 %collective-permute-done.3 = f32[104,128]{1,0:T(8,128)S(1)} collective-permute-done((f32[104,128]{1,0:T(8,128)S(1)}, f32[104,128]{1,0:T(8,128)S(1)}, u32[]{:S(2)}, u32[]{:S(2)}) %collective-permute-start.3) | collective-permute-done | bytes 53280 | tf_op jit(solution)/shard_map/ppermute | solution.py:426
  65.6 1.6 %collective-permute-start.4 = (f32[104,128]{1,0:T(8,128)S(1)}, f32[104,128]{1,0:T(8,128)S(1)}, u32[]{:S(2)}, u32[]{:S(2)}) collective-permute-start(f32[104,128]{1,0:T(8,128)S(1)} %add.18), channel_id=1, source_target_pairs={{0,4},{1,5},{2,6},{3,7},{4,0},{5,1},{6,2},{7,3},{8,12},{9,13},{10,... | collective-permute-start | bytes 159752 | tf_op jit(solution)/shard_map/ppermute | solution.py:426
  67.3 2.6 %collective-permute-done.4 = f32[104,128]{1,0:T(8,128)S(1)} collective-permute-done((f32[104,128]{1,0:T(8,128)S(1)}, f32[104,128]{1,0:T(8,128)S(1)}, u32[]{:S(2)}, u32[]{:S(2)}) %collective-permute-start.4) | collective-permute-done | bytes 53280 | tf_op jit(solution)/shard_map/ppermute | solution.py:426
  69.8 2.7 %collective-permute-start.5 = (f32[104,128]{1,0:T(8,128)S(1)}, f32[104,128]{1,0:T(8,128)S(1)}, u32[]{:S(2)}, u32[]{:S(2)}) collective-permute-start(f32[104,128]{1,0:T(8,128)S(1)} %add.19), channel_id=1, source_target_pairs={{0,8},{1,9},{2,10},{3,11},{4,12},{5,13},{6,14},{7,15},{8,0},{9,1},... | collective-permute-start | bytes 159752 | tf_op jit(solution)/shard_map/ppermute | solution.py:426
  72.5 2.4 %collective-permute-done.5 = f32[104,128]{1,0:T(8,128)S(1)} collective-permute-done((f32[104,128]{1,0:T(8,128)S(1)}, f32[104,128]{1,0:T(8,128)S(1)}, u32[]{:S(2)}, u32[]{:S(2)}) %collective-permute-start.5) | collective-permute-done | bytes 53280 | tf_op jit(solution)/shard_map/ppermute | solution.py:426
  75.0 0.1 collective-permute-start.6
  75.0 1.2 %collective-permute-done.6.refs_2_ = f32[104,128]{1,0:T(8,128)S(1)} collective-permute-done((f32[104,128]{1,0:T(8,128)S(1)}, f32[104,128]{1,0:T(8,128)S(1)}, u32[]{:S(2)}, u32[]{:S(2)}) %collective-permute-start.6) | collective-permute-done | bytes 53280 | tf_op jit(solution)/shard_map/ppermute | solution.py:426
  76.3 0.8 %shard_map.173 = (f32[32,256]{1,0:T(8,128)}, f32[64,256]{1,0:T(8,128)}, f32[1,256]{1,0:T(1,128)}, f32[2,64]{1,0:T(2,128)}, f32[1,2]{1,0:T(1,128)}, /*index=5*/f32[1,1]{1,0:T(1,128)}) custom-call(s32[1]{0:T(128)} %bitcast.refs_0_, f32[104,128]{1,0:T(8,128)S(1)} %add.20.refs_1_, f32[104,128]{1,0:T(8,128)S(1)} %collective-permute-done.6.refs_2_), custom_call_target="tpu_custom_call" | custom-call | tf_op jit(solution)/shard_map/pallas_call | solution.py:522
  (3 shorter events, 0.0 us)
Async XLA Ops:
  17.6 3.7 %collective-permute-start = (f32[84,256]{1,0:T(8,128)}, f32[84,256]{1,0:T(8,128)S(1)}, u32[]{:S(2)}, u32[]{:S(2)}) collective-permute-start(f32[84,256]{1,0:T(8,128)} %get-tuple-element.32), channel_id=1, source_target_pairs={{0,1},{1,2},{2,3},{3,4},{4,5},{5,6},{6,7},{7,8},{8,9},{9,10},{10,1... | collective-permute-start | bytes 258056 | tf_op jit(solution)/shard_map/ppermute | solution.py:479
  19.9 5.5 %collective-permute-start.1 = (f32[84,256]{1,0:T(8,128)}, f32[84,256]{1,0:T(8,128)S(1)}, u32[]{:S(2)}, u32[]{:S(2)}) collective-permute-start(f32[84,256]{1,0:T(8,128)} %get-tuple-element.33), channel_id=1, source_target_pairs={{1,0},{2,1},{3,2},{4,3},{5,4},{6,5},{7,6},{8,7},{9,8},{10,9},{11,1... | collective-permute-start | bytes 258056 | tf_op jit(solution)/shard_map/ppermute | solution.py:480
  21.2 4.2 %copy-start = (f32[84,256]{1,0:T(8,128)}, f32[84,256]{1,0:T(8,128)S(1)}, u32[]{:S(2)}) copy-start(f32[84,256]{1,0:T(8,128)S(1)} %collective-permute-done.refs_8_) | copy-start | bytes 258052
  25.4 0.6 copy-start.1
  55.7 4.3 %collective-permute-start.2 = (f32[104,128]{1,0:T(8,128)}, f32[104,128]{1,0:T(8,128)S(1)}, u32[]{:S(2)}, u32[]{:S(2)}) collective-permute-start(f32[104,128]{1,0:T(8,128)} %get-tuple-element.36), channel_id=1, source_target_pairs={{0,1},{1,0},{2,3},{3,2},{4,5},{5,4},{6,7},{7,6},{8,9},{9,8},{10,11... | collective-permute-start | bytes 159752 | tf_op jit(solution)/shard_map/ppermute | solution.py:426
  60.9 4.8 %collective-permute-start.3 = (f32[104,128]{1,0:T(8,128)S(1)}, f32[104,128]{1,0:T(8,128)S(1)}, u32[]{:S(2)}, u32[]{:S(2)}) collective-permute-start(f32[104,128]{1,0:T(8,128)S(1)} %add.17), channel_id=1, source_target_pairs={{0,2},{1,3},{2,0},{3,1},{4,6},{5,7},{6,4},{7,5},{8,10},{9,11},{10,... | collective-permute-start | bytes 159752 | tf_op jit(solution)/shard_map/ppermute | solution.py:426
  65.6 4.2 %collective-permute-start.4 = (f32[104,128]{1,0:T(8,128)S(1)}, f32[104,128]{1,0:T(8,128)S(1)}, u32[]{:S(2)}, u32[]{:S(2)}) collective-permute-start(f32[104,128]{1,0:T(8,128)S(1)} %add.18), channel_id=1, source_target_pairs={{0,4},{1,5},{2,6},{3,7},{4,0},{5,1},{6,2},{7,3},{8,12},{9,13},{10,... | collective-permute-start | bytes 159752 | tf_op jit(solution)/shard_map/ppermute | solution.py:426
  69.8 5.1 %collective-permute-start.5 = (f32[104,128]{1,0:T(8,128)S(1)}, f32[104,128]{1,0:T(8,128)S(1)}, u32[]{:S(2)}, u32[]{:S(2)}) collective-permute-start(f32[104,128]{1,0:T(8,128)S(1)} %add.19), channel_id=1, source_target_pairs={{0,8},{1,9},{2,10},{3,11},{4,12},{5,13},{6,14},{7,15},{8,0},{9,1},... | collective-permute-start | bytes 159752 | tf_op jit(solution)/shard_map/ppermute | solution.py:426
  75.0 1.3 %collective-permute-start.6 = (f32[104,128]{1,0:T(8,128)S(1)}, f32[104,128]{1,0:T(8,128)S(1)}, u32[]{:S(2)}, u32[]{:S(2)}) collective-permute-start(f32[104,128]{1,0:T(8,128)S(1)} %add.20.refs_1_), channel_id=1, source_target_pairs={{0,1},{1,0},{2,3},{3,2},{4,5},{5,4},{6,7},{7,6},{8,9},{9,8},{10,11... | collective-permute-start | bytes 159752 | tf_op jit(solution)/shard_map/ppermute | solution.py:426
